TPU v7x, 32 devices: a whole 2x2x4 slice. The times are simulated.
32 devices in a mesh: gx: 4 (over z), gy: 4 (over y, core), gz: 2 (over x).
Axes of the slice: x: 2, y: 2, z: 4, core: 2. Of those that a mesh axis runs over, the one named last changes fastest.
Arguments:
- offset_vector_field: float32 [3, 64, 64, 256], P(None, 'gx', 'gy', 'gz'), may hold values from -2 to 2
- earlier_creep_deformation: float32 [6, 64, 64, 256], P(None, 'gx', 'gy', 'gz'), may hold values from -0.6 to 0.6
- thermal_state: float32 [64, 64, 256], P('gx', 'gy', 'gz'), may hold values from 1 to 2
- rock_mass_per_volume: float32 [64, 64, 256], P('gx', 'gy', 'gz'), may hold values from 0.5 to 1.5
- rupture_band_indicator: int32 [64, 64, 256], P('gx', 'gy', 'gz'), may hold values 0 or 1
Outputs:
- strain_next: float32 [6, 64, 64, 256], P(None, 'gx', 'gy', 'gz')
- momentum_residual: float32 [3, 64, 64, 256], P(None, 'gx', 'gy', 'gz')
All inputs are finite; a program needn't handle non-finite values. No bound on the sum of `rupture_band_indicator` on one device may be relied on, other than what follows from the above.
Results may differ from a plain program's by a relative error of at most 0.00009.
Values sent between devices are 32-bit elements; how exact they have to be, the bound alone decides.
A program may use at most 64 MiB of HBM per device.

v0:
```python
import functools

import jax
import jax.numpy as jnp
from jax import lax
from jax.experimental import pallas as pl
from jax.experimental.pallas import tpu as pltpu
from jax.sharding import PartitionSpec as P

MESH = pl.DeviceIdType.MESH
AXES = ("gx", "gy", "gz")
X_SET = (0, 2, 1)
Y_SET = (2, 3, 4)
Z_SET = (1, 4, 5)


def merge(pairs, Z):
    low, high = pairs[0], pairs[1]
    even = (lax.broadcasted_iota(jnp.int32, low.shape, 1) & 1) == 0
    return jnp.where(even, low, pltpu.roll(high, Z - 2, 1))


def edge_term(tile, q, z_edge):
    Z = tile.shape[1]
    return (pltpu.roll(tile, (Z - 2 * q) % Z, 1) if q else tile) * z_edge


def kernel(
    dims, sizes,
    u_hbm, u_rows, e_hbm, t_hbm, r_hbm, b_hbm,
    fv, mv,
    uv, ev, tv, rv, bv, pv, el, nt, sp,
    yur, zus, zur, zts, ztr, xur, yss, ysr, zss, zsr, xsr,
    in_sem, x_send, x_recv, y_send, y_recv, z_send, z_recv, t_send, t_recv,
    x2_send, x2_recv, y2_send, y2_recv, z2_send, z2_recv,
):
    X, Y, Z = dims
    N = X * Y
    layers = sizes[2]
    me = [lax.axis_index(a) for a in AXES]
    has = [(me[a] > 0, me[a] < sizes[a] - 1) for a in range(3)]

    def to(axis, step):
        return {AXES[axis]: me[axis] + step}

    loads = [
        pltpu.make_async_copy(src, dst, in_sem.at[i])
        for i, (src, dst) in enumerate(
            (
                (u_hbm, uv.at[:, pl.ds(Y, N), :]),
                (r_hbm, rv),
                (e_hbm, ev),
                (t_hbm, tv),
                (b_hbm, bv),
            )
        )
    ]
    for copy in loads:
        copy.start()

    barrier = pltpu.get_barrier_semaphore()
    expected = jnp.int32(0)
    for axis in range(3):
        for side, step in enumerate((-1, 1)):
            expected = expected + has[axis][side].astype(jnp.int32)

            @pl.when(has[axis][side])
            def _(axis=axis, step=step):
                pl.semaphore_signal(barrier, inc=1, device_id=to(axis, step), device_id_type=MESH)

    for d in range(2, layers):
        expected = expected + (me[2] + d < layers).astype(jnp.int32)

        @pl.when(me[2] >= d)
        def _(d=d):
            pl.semaphore_signal(barrier, inc=1, device_id=to(2, -d), device_id_type=MESH)

    plane = jnp.zeros((Y, Z), jnp.float32)
    for c in range(3):
        uv[c, pl.ds(0, Y), :] = plane
        uv[c, pl.ds(Y + N, Y), :] = plane
    for c in range(6):
        sp[c, pl.ds(0, Y), :] = plane
        sp[c, pl.ds(Y + N, Y), :] = plane
    for d in range(1, layers):
        @pl.when(me[2] < d)
        def _(d=d):
            ztr[d - 1] = plane

    for side in range(2):
        @pl.when(jnp.logical_not(has[2][side]))
        def _(side=side):
            zur[side] = plane
            zsr[side] = plane

    lane = lax.broadcasted_iota(jnp.int32, (Y, Z), 1)
    row = lax.broadcasted_iota(jnp.int32, (Y, Z), 0)
    pair = lane >> 1
    not_last = jnp.where(row < Y - 1, 0.5, 0.0).astype(jnp.float32)
    not_first = jnp.where(row > 0, 0.5, 0.0).astype(jnp.float32)
    z_first = jnp.where(lane > 0, 0.5, 0.0).astype(jnp.float32)
    z_last = jnp.where(lane < Z - 1, 0.5, 0.0).astype(jnp.float32)
    z_edge = jnp.where(lane == 0, -0.5, jnp.where(lane == Z - 1, 0.5, 0.0)).astype(jnp.float32)

    def remote(src, dst, send, recv, axis, step):
        return pltpu.make_async_remote_copy(
            src_ref=src, dst_ref=dst, send_sem=send, recv_sem=recv,
            device_id=to(axis, step), device_id_type=MESH,
        )

    def start(copies):
        for sends, _, copy in copies:
            @pl.when(sends)
            def _(copy=copy):
                copy.start()

    def arrive(copies):
        for _, receives, copy in copies:
            @pl.when(receives)
            def _(copy=copy):
                copy.wait_recv()

    def faces(axis, src, dst, send, recv):
        return [
            (has[axis][side], has[axis][1 - side], remote(
                src[side], dst.at[1 - side], send.at[side], recv.at[1 - side], axis, step))
            for side, step in enumerate((-1, 1))
        ]

    edges = (pl.ds(Y, Y), pl.ds(Y * X, Y))
    u_x = faces(0, [u_hbm.at[:, pl.ds(at, Y), :] for at in (0, N - Y)], xur, x_send, x_recv)
    u_y = faces(1, [u_rows.at[:, :, y, :] for y in (0, Y - 1)], yur, y_send, y_recv)
    u_z = faces(2, [zus, zus], zur, z_send, z_recv)
    totals_down = [
        (me[2] + d < layers, me[2] >= d, remote(
            zts, ztr.at[d - 1], t_send.at[d - 1], t_recv.at[d - 1], 2, d))
        for d in range(1, layers)
    ]

    pl.semaphore_wait(barrier, expected)
    start(u_x + u_y)
    loads[0].wait()
    message = plane
    for x in range(X):
        for c in range(3):
            q = c * X + x
            tile = pltpu.roll(uv[c, pl.ds(Y + x * Y, Y), :], (2 * q + 1) % Z, 1)
            message = jnp.where(pair == q, tile, message)
    zus[...] = message
    start(u_z)

    loads[1].wait()
    total_depth = Z * layers
    depth = (me[2] * Z + lax.broadcasted_iota(jnp.int32, (N, Z), 1)).astype(jnp.float32)
    weight = rv[...] * (1.0 + 2.0 * depth / total_depth) / total_depth
    above_row = lax.broadcasted_iota(jnp.int32, (Z, 2 * Z), 0)
    column = lax.broadcasted_iota(jnp.int32, (Z, 2 * Z), 1)
    triangle = jnp.where(
        (above_row < column) | (column >= Z),
        1.0,
        jnp.where(above_row == column, 0.5, 0.0),
    ).astype(jnp.float32)
    sums = jnp.dot(
        weight, triangle, precision=lax.Precision.HIGHEST, preferred_element_type=jnp.float32
    )
    pv[...] = sums[:, :Z] + 1.0
    totals = sums[:, Z:]
    message = plane
    for x in range(X):
        message = jnp.where(lane == x, totals[x * Y:(x + 1) * Y], message)
    zts[...] = message
    start(totals_down)

    for copy in loads[2:]:
        copy.wait()
    for x in range(X):
        base = Y + x * Y
        own = pl.ds(x * Y, Y)
        grad = []
        for c in range(3):
            here = uv[c, pl.ds(base, Y), :]
            grad.append((
                (uv[c, pl.ds(base + Y, Y), :] - uv[c, pl.ds(base - Y, Y), :]) * 0.5,
                uv[c, pl.ds(base + 1, Y), :] * not_last - uv[c, pl.ds(base - 1, Y), :] * not_first,
                pltpu.roll(here, Z - 1, 1) * z_last - pltpu.roll(here, 1, 1) * z_first,
            ))
        el[0, own, :] = grad[0][0] - ev[0, own, :]
        el[1, own, :] = grad[1][1] - ev[1, own, :]
        el[2, own, :] = grad[2][2] - ev[2, own, :]
        el[3, own, :] = 0.5 * (grad[0][1] + grad[1][0]) - ev[3, own, :]
        el[4, own, :] = 0.5 * (grad[0][2] + grad[2][0]) - ev[4, own, :]
        el[5, own, :] = 0.5 * (grad[1][2] + grad[2][1]) - ev[5, own, :]
        nt[own, :] = -2.0 / tv[own, :]

    arrive(u_y)
    for side, line in enumerate((0, Y - 1)):
        sign = 2.0 * side - 1.0

        @pl.when(has[1][side])
        def _(side=side, sign=sign, line=line):
            own = pl.ds(line, X, stride=Y)
            for c, (part, factor) in enumerate(((3, 0.25), (1, 0.5), (5, 0.25))):
                el[part, own, :] = el[part, own, :] + (sign * factor) * yur[side, c]

    arrive(u_z + totals_down)
    carried = plane
    for d in range(1, layers):
        carried = carried + ztr[d - 1]
    merged = merge(zur, Z)

    s_x = faces(0, [sp.at[pl.ds(0, 3), edge, :] for edge in edges], xsr, x2_send, x2_recv)
    s_y = faces(1, [yss.at[0], yss.at[1]], ysr, y2_send, y2_recv)
    s_z = faces(2, [zss, zss], zsr, z2_send, z2_recv)

    def evolve(e, load, own):
        trace = e[0] + e[1] + e[2]
        third = trace * (1.0 / 3.0)
        half = [e[0] - third, e[1] - third, e[2] - third, e[3], e[4], e[5]]
        second = half[0] * half[0] + half[1] * half[1] + half[2] * half[2]
        second = second + 2.0 * (half[3] * half[3] + half[4] * half[4] + half[5] * half[5])
        weak = 2.0 + 14.0 * bv[own, :].astype(jnp.float32)
        rate = weak * jnp.exp(load * nt[own, :]) * second
        e = list(e)
        for c in range(6):
            change = rate * half[c]
            fv[c, own, :] = ev[c, own, :] + change
            e[c] = e[c] - change
        trace = e[0] + e[1] + e[2]
        return [
            2.0 * e[0] + trace, 2.0 * e[4], 2.0 * e[3],
            2.0 * e[1] + trace, 2.0 * e[5], 2.0 * e[2] + trace,
        ]

    def advance(x, message):
        own = pl.ds(x * Y, Y)
        e = [el[c, own, :] for c in range(6)]
        e[4] = e[4] + 0.5 * edge_term(merged, x, z_edge)
        e[5] = e[5] + 0.5 * edge_term(merged, X + x, z_edge)
        e[2] = e[2] + edge_term(merged, 2 * X + x, z_edge)
        load = pv[own, :] + jnp.broadcast_to(carried[:, x:x + 1], (Y, Z))
        stress = evolve(e, load, own)
        for c in range(6):
            sp[c, pl.ds(Y + x * Y, Y), :] = stress[c]
        for c in range(3):
            q = c * X + x
            tile = pltpu.roll(stress[Z_SET[c]], (2 * q + 1) % Z, 1)
            message = jnp.where(pair == q, tile, message)
        return message

    message = plane
    for x in range(1, X - 1):
        message = advance(x, message)
    arrive(u_x)
    for side, at in enumerate((0, X - 1)):
        sign = 2.0 * side - 1.0

        @pl.when(has[0][side])
        def _(side=side, sign=sign, at=at):
            own = pl.ds(at * Y, Y)
            for c, (part, factor) in enumerate(((0, 0.5), (3, 0.25), (4, 0.25))):
                el[part, own, :] = el[part, own, :] + (sign * factor) * xur[side, c]

    for x in sorted({0, X - 1}):
        message = advance(x, message)
    start(s_x)
    zss[...] = message
    start(s_z)
    for side, line in enumerate((0, Y - 1)):
        for c in range(3):
            yss[side, c] = sp[Y_SET[c], pl.ds(Y + line, X, stride=Y), :]
    start(s_y)

    for x in range(X):
        base = Y + x * Y
        own = pl.ds(x * Y, Y)
        for c in range(3):
            cx, cy, cz = X_SET[c], Y_SET[c], Z_SET[c]
            here = sp[cz, pl.ds(base, Y), :]
            total = (sp[cx, pl.ds(base + Y, Y), :] - sp[cx, pl.ds(base - Y, Y), :]) * 0.5
            total = total + (
                sp[cy, pl.ds(base + 1, Y), :] * not_last - sp[cy, pl.ds(base - 1, Y), :] * not_first
            )
            total = total + (pltpu.roll(here, Z - 1, 1) * z_last - pltpu.roll(here, 1, 1) * z_first)
            if c == 2:
                total = total - 0.5 * rv[own, :]
            mv[c, own, :] = total

    arrive(s_y)
    for side, line in enumerate((0, Y - 1)):
        @pl.when(has[1][side])
        def _(side=side, line=line):
            own = pl.ds(line, X, stride=Y)
            for c in range(3):
                mv[c, own, :] = mv[c, own, :] + (side - 0.5) * ysr[side, c]

    arrive(s_z)
    merged = merge(zsr, Z)
    for c in range(3):
        for x in range(X):
            own = pl.ds(x * Y, Y)
            mv[c, own, :] = mv[c, own, :] + edge_term(merged, c * X + x, z_edge)

    for sends, _, copy in u_x + u_y + u_z + totals_down + s_y + s_z:
        @pl.when(sends)
        def _(copy=copy):
            copy.wait_send()

    arrive(s_x)
    for side, at in enumerate((0, X - 1)):
        @pl.when(has[0][side])
        def _(side=side, at=at):
            own = pl.ds(at * Y, Y)
            for c in range(3):
                mv[c, own, :] = mv[c, own, :] + (side - 0.5) * xsr[side, X_SET[c]]

    for sends, _, copy in s_x:
        @pl.when(sends)
        def _(copy=copy):
            copy.wait_send()


def finish(fv, mv, f_hbm, m_hbm, sem):
    copies = [
        pltpu.make_async_copy(mv, m_hbm, sem.at[0]),
        pltpu.make_async_copy(fv, f_hbm, sem.at[1]),
    ]
    for copy in copies:
        copy.start()
    for copy in copies:
        copy.wait()


def shards(sizes, u, e, t, r, b):
    X, Y, Z = t.shape
    N = X * Y
    layers = sizes[2]
    assert 8 * X <= Z and Z % 128 == 0 and Y % 8 == 0
    f32 = jnp.float32
    vmem = pltpu.VMEM
    dma = pltpu.SemaphoreType.DMA
    any_space = pl.BlockSpec(memory_space=pl.ANY)
    in_vmem = pl.BlockSpec(memory_space=vmem)
    pair_sem = dma((2,))
    per_layer = dma((max(layers - 1, 1),))
    kept = pl.pallas_call(
        functools.partial(kernel, (X, Y, Z), sizes),
        out_shape=(vmem((6, N, Z), f32), vmem((3, N, Z), f32)),
        in_specs=[any_space] * 6,
        out_specs=(in_vmem, in_vmem),
        scratch_shapes=[
            vmem((3, N + 2 * Y, Z), f32),
            vmem((6, N, Z), f32),
            vmem((N, Z), f32),
            vmem((N, Z), f32),
            vmem((N, Z), jnp.int32),
            vmem((N, Z), f32),
            vmem((6, N, Z), f32),
            vmem((N, Z), f32),
            vmem((6, N + 2 * Y, Z), f32),
            vmem((2, 3, X, Z), f32),
            vmem((Y, Z), f32),
            vmem((2, Y, Z), f32),
            vmem((Y, Z), f32),
            vmem((max(layers - 1, 1), Y, Z), f32),
            vmem((2, 3, Y, Z), f32),
            vmem((2, 3, X, Z), f32),
            vmem((2, 3, X, Z), f32),
            vmem((Y, Z), f32),
            vmem((2, Y, Z), f32),
            vmem((2, 3, Y, Z), f32),
            dma((5,)),
        ] + [pair_sem] * 6 + [per_layer] * 2 + [pair_sem] * 6,
        compiler_params=pltpu.CompilerParams(collective_id=0, has_side_effects=True),
        name="strain_step",
    )(
        u.reshape(3, N, Z), u, e.reshape(6, N, Z), t.reshape(N, Z), r.reshape(N, Z), b.reshape(N, Z)
    )
    f, m = pl.pallas_call(
        finish,
        out_shape=(jax.ShapeDtypeStruct((6, N, Z), f32), jax.ShapeDtypeStruct((3, N, Z), f32)),
        in_specs=[in_vmem] * 2,
        out_specs=(any_space, any_space),
        scratch_shapes=[pair_sem],
        name="finish",
    )(*(pltpu.with_memory_space_constraint(k, vmem) for k in kept))
    return f.reshape(6, X, Y, Z), m.reshape(3, X, Y, Z)


def solution(mesh):
    sizes = tuple(mesh.shape[a] for a in AXES)
    field = P("gx", "gy", "gz")
    fields = P(None, "gx", "gy", "gz")
    return jax.shard_map(
        functools.partial(shards, sizes),
        mesh=mesh,
        in_specs=(fields, fields, field, field, field),
        out_specs=(fields, fields),
        check_vma=False,
    )
```

profile of v0, /device:TPU:0, one launch (start us, length us, event | category | flops | bytes accessed | tf_op | source)
XLA Modules:
  0.0 12.4 jit_solution(1824642687748364780)
XLA Ops:
  0.6 10.7 %strain_step.1 = (f32[6,256,128]{2,1,0:T(8,128)S(1)}, f32[3,256,128]{2,1,0:T(8,128)S(1)}) custom-call(f32[3,256,128]{2,1,0:T(8,128)} %bitcast.7, f32[3,16,16,128]{3,2,1,0:T(8,128)} %u_rows.1, f32[6,256,128]{2,1,0:T(8,128)} %bitcast.8, f32[256,128]{1,0:T(8,128)} %bitcast.9, f32[256,128]{1,0:T(8,128)} %bitcast.10, s32[256,128]{1,0:T(8,128)} %bitcast.11), custom_call_target="tpu_custom_call" | custom-call | tf_op jit(solution)/shard_map/strain_step/pallas_call | solution.py:345
  11.4 1.0 %finish.1 = (f32[6,256,128]{2,1,0:T(8,128)}, f32[3,256,128]{2,1,0:T(8,128)}) custom-call(f32[6,256,128]{2,1,0:T(8,128)S(1)} %get-tuple-element.6.fv, f32[3,256,128]{2,1,0:T(8,128)S(1)} %get-tuple-element.7.mv), custom_call_target="tpu_custom_call" | custom-call | tf_op jit(solution)/shard_map/finish/pallas_call | solution.py:378
where the time goes:
time: 12.6 us; the launch traced here: 12.4 us
  Pallas kernels  11.8 us (94%)
  between operations  0.64 us (5%)
    pallas_call x1, Pallas kernels, shards(): pl.pallas_call(functools.partial(kernel, (X, Y, Z), sizes), out_shape=(vm...  10.7 us
    pallas_call x1, Pallas kernels, shards(): pl.pallas_call(finish, out_shape=(jax.ShapeDtypeStruct((6, N, Z), f32), j...  1.03 us

commit v1 on v0

v1 whole, which is shorter than its diff:
```python
import functools

import jax
import jax.numpy as jnp
from jax import lax
from jax.experimental import pallas as pl
from jax.experimental.pallas import tpu as pltpu
from jax.sharding import PartitionSpec as P

MESH = pl.DeviceIdType.MESH
AXES = ("gx", "gy", "gz")
ORDER = (2, 1, 0)
TERMS = (
    ((0, 0.5), (3, 0.25), (4, 0.25)),
    ((3, 0.25), (1, 0.5), (5, 0.25)),
    ((4, 0.25), (5, 0.25), (2, 0.5)),
)
X_SET = (0, 3, 4)
Y_SET = (3, 1, 5)
Z_SET = (4, 5, 2)


def upper(o):
    return tuple(o[a] for a in ORDER) > (0, 0, 0)


def offsets(layers):
    near = [
        (x, y, z)
        for x in (-1, 0, 1)
        for y in (-1, 0, 1)
        for z in (-1, 0, 1)
        if 1 <= abs(x) + abs(y) + abs(z) <= 2
    ]
    far = [
        (x, y, s * d)
        for d in range(2, layers)
        for s in (-1, 1)
        for x, y in ((0, 0), (-1, 0), (1, 0), (0, -1), (0, 1))
    ]
    return near + far


def minus(o):
    return tuple(-v for v in o)


def merge(low, high):
    Z = low.shape[1]
    even = (lax.broadcasted_iota(jnp.int32, low.shape, 1) & 1) == 0
    return jnp.where(even, low, pltpu.roll(high, Z - 2, 1))


def edge_term(tile, q, z_edge):
    Z = tile.shape[1]
    return (pltpu.roll(tile, (Z - 2 * q) % Z, 1) if q else tile) * z_edge


def flow(e, pace):
    trace = e[0] + e[1] + e[2]
    third = trace * (1.0 / 3.0)
    half = [e[0] - third, e[1] - third, e[2] - third, e[3], e[4], e[5]]
    second = half[0] * half[0] + half[1] * half[1] + half[2] * half[2]
    second = second + 2.0 * (half[3] * half[3] + half[4] * half[4] + half[5] * half[5])
    rate = pace * second
    return trace, [rate * h for h in half]


def stress(e, change, trace, part):
    out = 2.0 * (e[part] - change[part])
    return out + trace if part < 3 else out


def kernel(
    dims, sizes,
    u_hbm, e_hbm, t_hbm, r_hbm, b_hbm,
    fv, mv,
    uv, ev, tv, rv, bv, pv, tot, el, av, nt, sp,
    xs, ys, yu, zu, zs, xy, zt, xt, yt,
    rxu, rxs, ryu, rys, rzu, rzs, rxy, rxz, ryz, rt, rtx, rty,
    in_sem, ready,
    xu_send, xu_recv, xs_send, xs_recv, yu_send, yu_recv, ys_send, ys_recv,
    zu_send, zu_recv, zs_send, zs_recv, xy_send, xy_recv, xz_send, xz_recv, yz_send, yz_recv,
    t_send, t_recv, tx_send, tx_recv, ty_send, ty_recv,
):
    X, Y, Z = dims
    N = X * Y
    layers = sizes[2]
    depths = range(1, layers)
    me = [lax.axis_index(a) for a in AXES]
    offs = offsets(layers)
    uppers = [o for o in offs if upper(o)]
    lowers = [o for o in offs if not upper(o)]

    def exists(o):
        ok = None
        for a in range(3):
            if o[a]:
                here = me[a] + o[a]
                test = here < sizes[a] if o[a] > 0 else here >= 0
                ok = test if ok is None else jnp.logical_and(ok, test)
        return ok

    def partner(o):
        return {AXES[a]: me[a] + o[a] for a in range(3) if o[a]}

    has = {o: exists(o) for o in offs}
    faces = {a: [tuple(s if i == a else 0 for i in range(3)) for s in (-1, 1)] for a in range(3)}

    loads = [
        pltpu.make_async_copy(src, dst, in_sem.at[i])
        for i, (src, dst) in enumerate(
            (
                (u_hbm, uv.at[:, pl.ds(Y, N), :]),
                (r_hbm, rv),
                (t_hbm, tv),
                (b_hbm, bv),
                (e_hbm, ev),
            )
        )
    ]
    for copy in loads:
        copy.start()

    barrier = pltpu.get_barrier_semaphore()
    for o in uppers:
        @pl.when(has[o])
        def _(o=o):
            pl.semaphore_signal(barrier, inc=1, device_id=partner(o), device_id_type=MESH)
    expected = jnp.int32(0)
    for o in lowers:
        expected = expected + has[o].astype(jnp.int32)

    plane = jnp.zeros((Y, Z), jnp.float32)
    row_plane = jnp.zeros((X, Z), jnp.float32)
    for c in range(3):
        uv[c, pl.ds(0, Y), :] = plane
        uv[c, pl.ds(Y + N, Y), :] = plane
    for c in range(6):
        sp[c, pl.ds(0, Y), :] = plane
        sp[c, pl.ds(Y + N, Y), :] = plane

    def blank(o, *refs):
        @pl.when(jnp.logical_not(has[o]))
        def _():
            for ref in refs:
                ref[...] = jnp.zeros(ref.shape, jnp.float32)

    for i, sz in enumerate((-1, 1)):
        blank((0, 0, sz), rzu.at[i], rzs.at[i])
        for j, s in enumerate((-1, 1)):
            blank((s, 0, sz), rxz.at[j, i])
            blank((0, s, sz), ryz.at[j, i])
    for i, sx in enumerate((-1, 1)):
        for j, sy in enumerate((-1, 1)):
            blank((sx, sy, 0), rxy.at[i, j])
    for d in depths:
        blank((0, 0, -d), rt.at[d - 1])
        for j, s in enumerate((-1, 1)):
            blank((s, 0, -d), rtx.at[j, d - 1])
            blank((0, s, -d), rty.at[j, d - 1])

    lane = lax.broadcasted_iota(jnp.int32, (Y, Z), 1)
    row = lax.broadcasted_iota(jnp.int32, (Y, Z), 0)
    pair = lane >> 1
    even = (lane & 1) == 0
    not_last = jnp.where(row < Y - 1, 0.5, 0.0).astype(jnp.float32)
    not_first = jnp.where(row > 0, 0.5, 0.0).astype(jnp.float32)
    z_first = jnp.where(lane > 0, 0.5, 0.0).astype(jnp.float32)
    z_last = jnp.where(lane < Z - 1, 0.5, 0.0).astype(jnp.float32)
    z_edge = jnp.where(lane == 0, -0.5, jnp.where(lane == Z - 1, 0.5, 0.0)).astype(jnp.float32)
    if X == Y:
        row_x, z_edge_x = row, z_edge
    else:
        lane_x = lax.broadcasted_iota(jnp.int32, (X, Z), 1)
        row_x = lax.broadcasted_iota(jnp.int32, (X, Z), 0)
        z_edge_x = jnp.where(lane_x == 0, -0.5, jnp.where(lane_x == Z - 1, 0.5, 0.0)).astype(jnp.float32)

    sends = {o: [] for o in offs}
    recvs = {}

    def message(kind, o, src, dst, send, recv):
        copy = pltpu.make_async_remote_copy(
            src_ref=src, dst_ref=dst, send_sem=send, recv_sem=recv,
            device_id=partner(o), device_id_type=MESH,
        )
        sends[o].append((kind, copy))
        recvs[kind, minus(o)] = copy

    for i, s in enumerate((-1, 1)):
        k = 1 - i
        at = (Y, Y * X)[i]
        message("xu", (s, 0, 0), uv.at[:, pl.ds(at, Y), :], rxu.at[k], xu_send.at[i], xu_recv.at[k])
        message("xs", (s, 0, 0), xs.at[i], rxs.at[k], xs_send.at[i], xs_recv.at[k])
        message("yu", (0, s, 0), yu.at[i], ryu.at[k], yu_send.at[i], yu_recv.at[k])
        message("ys", (0, s, 0), ys.at[i], rys.at[k], ys_send.at[i], ys_recv.at[k])
        message("zu", (0, 0, s), zu.at[0, pl.ds(0, Y)], rzu.at[k], zu_send.at[i], zu_recv.at[k])
        message("zs", (0, 0, s), zs, rzs.at[k], zs_send.at[i], zs_recv.at[k])
        for j, s2 in enumerate((-1, 1)):
            m = 1 - j
            message("xy", (s, s2, 0), xy.at[i, j], rxy.at[k, m], xy_send.at[i, j], xy_recv.at[k, m])
            message("xz", (s, 0, s2), zu.at[0, pl.ds(0, Y)], rxz.at[k, m], xz_send.at[i, j], xz_recv.at[k, m])
            message("yz", (0, s, s2), zu, ryz.at[k, m], yz_send.at[i, j], yz_recv.at[k, m])
        for d in depths:
            message("tx", (s, 0, d), xt.at[i], rtx.at[k, d - 1], tx_send.at[i, d - 1], tx_recv.at[k, d - 1])
            message("ty", (0, s, d), yt.at[i], rty.at[k, d - 1], ty_send.at[i, d - 1], ty_recv.at[k, d - 1])
    for d in depths:
        message("t", (0, 0, d), zt, rt.at[d - 1], t_send.at[d - 1], t_recv.at[d - 1])

    def start(offsets_in, kinds):
        for o in offsets_in:
            chosen = [copy for kind, copy in sends[o] if kind in kinds]
            if chosen:
                @pl.when(has[o])
                def _(chosen=chosen):
                    for copy in chosen:
                        copy.start()

    def arrive(*kinds):
        for (kind, o), copy in recvs.items():
            if kind in kinds:
                @pl.when(has[o])
                def _(copy=copy):
                    copy.wait_recv()

    loads[0].wait()
    tile0 = plane
    for x in range(X):
        for c in range(3):
            q = c * X + x
            tile = pltpu.roll(uv[c, pl.ds(Y + x * Y, Y), :], (2 * q + 1) % Z, 1)
            tile0 = jnp.where(pair == q, tile, tile0)
    zu[0, pl.ds(0, Y), :] = tile0
    tile = row_plane
    pair_x = lax.broadcasted_iota(jnp.int32, (X, Z), 1) >> 1
    for i, line in enumerate((0, Y - 1)):
        for c in range(3):
            p = 3 * i + c
            lines = uv[c, pl.ds(Y + line, X, stride=Y), :]
            yu[i, c] = lines
            tile = jnp.where(pair_x == p, pltpu.roll(lines, (2 * p + 1) % Z, 1), tile)
            for j, at in enumerate((0, X - 1)):
                xy[j, i, pl.ds(c, 1), :] = uv[c, pl.ds(Y + at * Y + line, 1), :]
    zu[1, pl.ds(0, X), :] = tile

    loads[1].wait()
    total_depth = Z * layers
    depth = (me[2] * Z + lane).astype(jnp.float32)
    scale = (1.0 + 2.0 * depth / total_depth) / total_depth
    weight = jnp.concatenate([rv[pl.ds(x * Y, Y), :] * scale for x in range(X)], axis=0)
    above_row = lax.broadcasted_iota(jnp.int32, (Z, 2 * Z), 0)
    column = lax.broadcasted_iota(jnp.int32, (Z, 2 * Z), 1)
    triangle = jnp.where(
        (above_row < column) | (column >= Z),
        1.0,
        jnp.where(above_row == column, 0.5, 0.0),
    ).astype(jnp.float32)
    sums = jnp.dot(
        weight, triangle, precision=lax.Precision.HIGHEST, preferred_element_type=jnp.float32
    )
    pv[...] = sums[:, :Z] + 1.0
    tot[...] = sums[:, Z:]
    tile = plane
    for x in range(X):
        tile = jnp.where(pair == x, tot[pl.ds(x * Y, Y), :], tile)
    zt[...] = tile
    for i, (at, line) in enumerate(((0, 0), (X - 1, Y - 1))):
        xt[i] = tot[pl.ds(at * Y, Y), :]
        yt[i] = tot[pl.ds(line, X, stride=Y), :]

    for copy in loads[2:]:
        copy.wait()
    tiles = [plane, plane]

    def local(x, tiles):
        base = Y + x * Y
        own = pl.ds(x * Y, Y)
        grad = []
        for c in range(3):
            here = uv[c, pl.ds(base, Y), :]
            grad.append((
                (uv[c, pl.ds(base + Y, Y), :] - uv[c, pl.ds(base - Y, Y), :]) * 0.5,
                uv[c, pl.ds(base + 1, Y), :] * not_last - uv[c, pl.ds(base - 1, Y), :] * not_first,
                pltpu.roll(here, Z - 1, 1) * z_last - pltpu.roll(here, 1, 1) * z_first,
            ))
        minus_two = -2.0 / tv[own, :]
        parts = [
            grad[0][0] - ev[0, own, :],
            grad[1][1] - ev[1, own, :],
            grad[2][2] - ev[2, own, :],
            0.5 * (grad[0][1] + grad[1][0]) - ev[3, own, :],
            0.5 * (grad[0][2] + grad[2][0]) - ev[4, own, :],
            0.5 * (grad[1][2] + grad[2][1]) - ev[5, own, :],
            (2.0 + 14.0 * bv[own, :].astype(jnp.float32)) * jnp.exp(pv[own, :] * minus_two),
            minus_two,
        ]
        for k in range(6):
            el[k, own, :] = parts[k]
        av[own, :] = parts[6]
        nt[own, :] = parts[7]
        for i, at in enumerate((0, X - 1)):
            if x == at:
                for k in range(8):
                    xs[i, k] = parts[k]
        tiles = list(tiles)
        for k in range(8):
            q = (k % 4) * X + x
            tile = pltpu.roll(parts[k], (2 * q + 1) % Z, 1)
            tiles[k // 4] = jnp.where(pair == q, tile, tiles[k // 4])
        return tiles

    ends = sorted({0, X - 1})
    for x in ends:
        tiles = local(x, tiles)

    @pl.when(expected > 0)
    def _():
        pl.semaphore_wait(barrier, expected)

    for o in lowers:
        @pl.when(has[o])
        def _(o=o):
            pl.semaphore_signal(
                ready.at[uppers.index(minus(o))], inc=1, device_id=partner(o), device_id_type=MESH
            )
    early = ("xu", "xs", "yu", "zu", "xy", "xz", "yz", "t", "tx", "ty")
    start(lowers, early)

    for x in range(X):
        if x not in ends:
            tiles = local(x, tiles)
    for i, line in enumerate((0, Y - 1)):
        for k in range(8):
            src = el.at[k] if k < 6 else (av, nt)[k - 6]
            ys[i, k] = src[pl.ds(line, X, stride=Y), :]
    start(lowers, ("ys",))
    for k in range(2):
        zs[k] = tiles[k]
    start(lowers, ("zs",))

    for o in uppers:
        @pl.when(has[o])
        def _(o=o):
            pl.semaphore_wait(ready.at[uppers.index(o)], 1)
    start(uppers, early + ("ys", "zs"))

    arrive("yu")
    for side, line in enumerate((0, Y - 1)):
        sign = 2.0 * side - 1.0

        @pl.when(has[faces[1][side]])
        def _(side=side, sign=sign, line=line):
            own = pl.ds(line, X, stride=Y)
            for c, (part, factor) in enumerate(TERMS[1]):
                el[part, own, :] = el[part, own, :] + (sign * factor) * ryu[side, c]

    arrive("zu", "t")
    carried = plane
    for d in depths:
        carried = carried + rt[d - 1]
    merged = merge(rzu[0], rzu[1])

    def advance(x):
        own = pl.ds(x * Y, Y)
        e = [el[c, own, :] for c in range(6)]
        for c, (part, factor) in enumerate(TERMS[2]):
            e[part] = e[part] + (2.0 * factor) * edge_term(merged, c * X + x, z_edge)
        load = jnp.broadcast_to(carried[:, 2 * x:2 * x + 1], (Y, Z))
        trace, change = flow(e, av[own, :] * jnp.exp(load * nt[own, :]))
        for c in range(6):
            fv[c, own, :] = ev[c, own, :] + change[c]
            sp[c, pl.ds(Y + x * Y, Y), :] = stress(e, change, trace, c)

    for x in range(X):
        if x not in ends:
            advance(x)
    arrive("xu")
    for side, at in enumerate((0, X - 1)):
        sign = 2.0 * side - 1.0

        @pl.when(has[faces[0][side]])
        def _(side=side, sign=sign, at=at):
            own = pl.ds(at * Y, Y)
            for c, (part, factor) in enumerate(TERMS[0]):
                el[part, own, :] = el[part, own, :] + (sign * factor) * rxu[side, c]

    for x in ends:
        advance(x)

    for x in range(X):
        base = Y + x * Y
        own = pl.ds(x * Y, Y)
        for c in range(3):
            cx, cy, cz = X_SET[c], Y_SET[c], Z_SET[c]
            here = sp[cz, pl.ds(base, Y), :]
            total = (sp[cx, pl.ds(base + Y, Y), :] - sp[cx, pl.ds(base - Y, Y), :]) * 0.5
            total = total + (
                sp[cy, pl.ds(base + 1, Y), :] * not_last - sp[cy, pl.ds(base - 1, Y), :] * not_first
            )
            total = total + (pltpu.roll(here, Z - 1, 1) * z_last - pltpu.roll(here, 1, 1) * z_first)
            if c == 2:
                total = total - 0.5 * rv[own, :]
            mv[c, own, :] = total

    def add(e, axis, factor, values):
        for c, (part, f) in enumerate(TERMS[axis]):
            e[part] = e[part] + (factor * f) * values[c]

    def ends_of(first, last, rows, count):
        return jnp.where(rows == 0, -first, jnp.where(rows == count - 1, last, 0.0))

    arrive("ys", "xy", "yz", "ty")
    for side, line in enumerate((0, Y - 1)):
        @pl.when(has[faces[1][side]])
        def _(side=side, line=line):
            e = [rys[side, k] for k in range(6)]
            add(e, 1, 1.0 - 2.0 * side, [uv[c, pl.ds(Y + line, X, stride=Y), :] for c in range(3)])
            add(e, 0, 1.0, [
                ends_of(rxy[0, side, pl.ds(c, 1), :], rxy[1, side, pl.ds(c, 1), :], row_x, X) for c in range(3)
            ])
            joined = merge(ryz[side, 0, 1, pl.ds(0, X), :], ryz[side, 1, 1, pl.ds(0, X), :])
            add(e, 2, 2.0, [edge_term(joined, 3 * (1 - side) + c, z_edge_x) for c in range(3)])
            load = row_plane
            for d in depths:
                load = load + rty[side, d - 1]
            trace, change = flow(e, rys[side, 6] * jnp.exp(load * rys[side, 7]))
            own = pl.ds(line, X, stride=Y)
            for c in range(3):
                mv[c, own, :] = mv[c, own, :] + (side - 0.5) * stress(e, change, trace, Y_SET[c])

    arrive("zs", "xz")
    block = 2 * X

    def shift(tile, by):
        return pltpu.roll(tile, by % Z, 1) if by % Z else tile

    halo = [jnp.where(even, rzs[0, k], rzs[1, k]) for k in range(2)]
    parts = [shift(halo[k // 4], -(k % 4) * block) for k in range(8)]
    mine = zu[0, pl.ds(0, Y), :]
    from_z = jnp.where(even, shift(mine, -1), -shift(mine, 1))
    left = jnp.where(even, rxz[0, 0], rxz[0, 1])
    right = jnp.where(even, rxz[1, 0], rxz[1, 1])
    spot = pair % X
    from_x = jnp.where(
        spot == 0, -shift(left, -2 * (X - 1)), jnp.where(spot == X - 1, shift(right, 2 * (X - 1)), 0.0)
    )
    even_row = (lax.broadcasted_iota(jnp.int32, (1, Z), 1) & 1) == 0
    from_y = ends_of(
        jnp.where(even_row, ryz[0, 0, 0, pl.ds(Y - 1, 1), :], ryz[0, 1, 0, pl.ds(Y - 1, 1), :]),
        jnp.where(even_row, ryz[1, 0, 0, pl.ds(0, 1), :], ryz[1, 1, 0, pl.ds(0, 1), :]),
        row, Y,
    )
    e = list(parts[:6])
    for axis, tile in enumerate((from_x, from_y, from_z)):
        add(e, axis, 1.0, [shift(tile, -c * block) for c in range(3)])
    deeper = plane
    for d in depths:
        if d >= 2:
            deeper = deeper + rt[d - 1]
    load = jnp.where(even, deeper, carried + zt[...])
    trace, change = flow(e, parts[6] * jnp.exp(load * parts[7]))
    known = jnp.where(
        even,
        has[0, 0, -1].astype(jnp.float32),
        has[0, 0, 1].astype(jnp.float32),
    )
    gathered = plane
    for c in range(3):
        tile = shift(stress(e, change, trace, Z_SET[c]) * known, c * block)
        gathered = jnp.where((pair >= c * X) & (pair < (c + 1) * X), tile, gathered)
    joined = jnp.where(even, gathered, shift(gathered, -2))
    for c in range(3):
        for x in range(X):
            own = pl.ds(x * Y, Y)
            mv[c, own, :] = mv[c, own, :] + edge_term(joined, c * X + x, z_edge)

    arrive("xs", "tx")
    for side, at in enumerate((0, X - 1)):
        @pl.when(has[faces[0][side]])
        def _(side=side, at=at):
            e = [rxs[side, k] for k in range(6)]
            add(e, 0, 1.0 - 2.0 * side, [uv[c, pl.ds(Y + at * Y, Y), :] for c in range(3)])
            add(e, 1, 1.0, [
                ends_of(rxy[side, 0, pl.ds(c, 1), :], rxy[side, 1, pl.ds(c, 1), :], row, Y) for c in range(3)
            ])
            facing = (X - 1) * (1 - side)
            joined = merge(rxz[side, 0], rxz[side, 1])
            add(e, 2, 2.0, [edge_term(joined, c * X + facing, z_edge) for c in range(3)])
            load = plane
            for d in depths:
                load = load + rtx[side, d - 1]
            trace, change = flow(e, rxs[side, 6] * jnp.exp(load * rxs[side, 7]))
            own = pl.ds(at * Y, Y)
            for c in range(3):
                mv[c, own, :] = mv[c, own, :] + (side - 0.5) * stress(e, change, trace, X_SET[c])

    for o in offs:
        if sends[o]:
            @pl.when(has[o])
            def _(o=o):
                for _, copy in sends[o]:
                    copy.wait_send()


def finish(fv, mv, f_hbm, m_hbm, sem):
    copies = [
        pltpu.make_async_copy(mv, m_hbm, sem.at[0]),
        pltpu.make_async_copy(fv, f_hbm, sem.at[1]),
    ]
    for copy in copies:
        copy.start()
    for copy in copies:
        copy.wait()


def shards(sizes, u, e, t, r, b):
    X, Y, Z = t.shape
    N = X * Y
    layers = sizes[2]
    assert 8 * X <= Z and Z % 128 == 0 and Y % 8 == 0 and X % 8 == 0
    W = max(X, Y)
    f32 = jnp.float32
    vmem = pltpu.VMEM
    dma = pltpu.SemaphoreType.DMA
    any_space = pl.BlockSpec(memory_space=pl.ANY)
    in_vmem = pl.BlockSpec(memory_space=vmem)
    D = max(layers - 1, 1)
    n_upper = sum(upper(o) for o in offsets(layers))
    kept = pl.pallas_call(
        functools.partial(kernel, (X, Y, Z), sizes),
        out_shape=(vmem((6, N, Z), f32), vmem((3, N, Z), f32)),
        in_specs=[any_space] * 5,
        out_specs=(in_vmem, in_vmem),
        scratch_shapes=[
            vmem((3, N + 2 * Y, Z), f32),
            vmem((6, N, Z), f32),
            vmem((N, Z), f32),
            vmem((N, Z), f32),
            vmem((N, Z), jnp.int32),
            vmem((N, Z), f32),
            vmem((N, Z), f32),
            vmem((6, N, Z), f32),
            vmem((N, Z), f32),
            vmem((N, Z), f32),
            vmem((6, N + 2 * Y, Z), f32),
            vmem((2, 8, Y, Z), f32),
            vmem((2, 8, X, Z), f32),
            vmem((2, 3, X, Z), f32),
            vmem((2, W, Z), f32),
            vmem((2, Y, Z), f32),
            vmem((2, 2, 8, Z), f32),
            vmem((Y, Z), f32),
            vmem((2, Y, Z), f32),
            vmem((2, X, Z), f32),
            vmem((2, 3, Y, Z), f32),
            vmem((2, 8, Y, Z), f32),
            vmem((2, 3, X, Z), f32),
            vmem((2, 8, X, Z), f32),
            vmem((2, Y, Z), f32),
            vmem((2, 2, Y, Z), f32),
            vmem((2, 2, 8, Z), f32),
            vmem((2, 2, Y, Z), f32),
            vmem((2, 2, 2, W, Z), f32),
            vmem((D, Y, Z), f32),
            vmem((2, D, Y, Z), f32),
            vmem((2, D, X, Z), f32),
            dma((5,)),
            pltpu.SemaphoreType.REGULAR((n_upper,)),
        ] + [dma((2,))] * 12 + [dma((2, 2))] * 6 + [dma((D,))] * 2 + [dma((2, D))] * 4,
        compiler_params=pltpu.CompilerParams(collective_id=0, has_side_effects=True),
        name="strain_step",
    )(u.reshape(3, N, Z), e.reshape(6, N, Z), t.reshape(N, Z), r.reshape(N, Z), b.reshape(N, Z))
    f, m = pl.pallas_call(
        finish,
        out_shape=(jax.ShapeDtypeStruct((6, N, Z), f32), jax.ShapeDtypeStruct((3, N, Z), f32)),
        in_specs=[in_vmem] * 2,
        out_specs=(any_space, any_space),
        scratch_shapes=[dma((2,))],
        name="finish",
    )(*(pltpu.with_memory_space_constraint(k, vmem) for k in kept))
    return f.reshape(6, X, Y, Z), m.reshape(3, X, Y, Z)


def solution(mesh):
    sizes = tuple(mesh.shape[a] for a in AXES)
    field = P("gx", "gy", "gz")
    fields = P(None, "gx", "gy", "gz")
    return jax.shard_map(
        functools.partial(shards, sizes),
        mesh=mesh,
        in_specs=(fields, fields, field, field, field),
        out_specs=(fields, fields),
        check_vma=False,
    )
```

time: 12.6 us -> 11.8 us (0.937)
  the two profiles are of different devices: /device:TPU:0 before, /device:TPU:1 now
where the time goes in v1:
time: 11.8 us; the launch traced here: 11.7 us
  Pallas kernels  11.1 us (94%)
  between operations  0.64 us (5%)
    pallas_call x1, Pallas kernels, shards(): pl.pallas_call(functools.partial(kernel, (X, Y, Z), sizes), out_shape=(vm...  10 us
    pallas_call x1, Pallas kernels, shards(): pl.pallas_call(finish, out_shape=(jax.ShapeDtypeStruct((6, N, Z), f32), j...  1.03 us

profile of v1, /device:TPU:1, one launch (start us, length us, event | category | flops | bytes accessed | tf_op | source)
XLA Modules:
  0.0 11.7 jit_solution(1557095925197021740)
XLA Ops:
  0.6 10.0 %strain_step.1 = (f32[6,256,128]{2,1,0:T(8,128)S(1)}, f32[3,256,128]{2,1,0:T(8,128)S(1)}) custom-call(f32[3,256,128]{2,1,0:T(8,128)} %bitcast.8, f32[6,256,128]{2,1,0:T(8,128)} %bitcast.7, f32[256,128]{1,0:T(8,128)} %bitcast.9, f32[256,128]{1,0:T(8,128)} %bitcast.10, s32[256,128]{1,0:T(8,128)} %bitcast.11), custom_call_target="tpu_custom_call" | custom-call | tf_op jit(solution)/shard_map/strain_step/pallas_call | solution.py:529
  10.7 1.0 %finish.1 = (f32[6,256,128]{2,1,0:T(8,128)}, f32[3,256,128]{2,1,0:T(8,128)}) custom-call(f32[6,256,128]{2,1,0:T(8,128)S(1)} %get-tuple-element.6.fv, f32[3,256,128]{2,1,0:T(8,128)S(1)} %get-tuple-element.7.mv), custom_call_target="tpu_custom_call" | custom-call | tf_op jit(solution)/shard_map/finish/pallas_call | solution.py:573

commit v2 on v1

--- a/solution.py
+++ b/solution.py
@@ -113,9 +113,11 @@
             (
                 (u_hbm, uv.at[:, pl.ds(Y, N), :]),
                 (r_hbm, rv),
+                (e_hbm.at[:, pl.ds(0, Y), :], ev.at[:, pl.ds(0, Y), :]),
+                (e_hbm.at[:, pl.ds(N - Y, Y), :], ev.at[:, pl.ds(N - Y, Y), :]),
                 (t_hbm, tv),
                 (b_hbm, bv),
-                (e_hbm, ev),
+                (e_hbm.at[:, pl.ds(Y, N - 2 * Y), :], ev.at[:, pl.ds(Y, N - 2 * Y), :]),
             )
         )
     ]
@@ -243,21 +245,40 @@
                 xy[j, i, pl.ds(c, 1), :] = uv[c, pl.ds(Y + at * Y + line, 1), :]
     zu[1, pl.ds(0, X), :] = tile
 
+    @pl.when(expected > 0)
+    def _():
+        pl.semaphore_wait(barrier, expected)
+
+    for o in lowers:
+        @pl.when(has[o])
+        def _(o=o):
+            pl.semaphore_signal(
+                ready.at[uppers.index(minus(o))], inc=1, device_id=partner(o), device_id_type=MESH
+            )
+    first = ("xu", "yu", "zu", "xy", "xz", "yz")
+    start(lowers, first)
+
     loads[1].wait()
     total_depth = Z * layers
     depth = (me[2] * Z + lane).astype(jnp.float32)
     scale = (1.0 + 2.0 * depth / total_depth) / total_depth
-    weight = jnp.concatenate([rv[pl.ds(x * Y, Y), :] * scale for x in range(X)], axis=0)
+    thirds = [[], [], []]
+    for x in range(X):
+        rest = rv[pl.ds(x * Y, Y), :] * scale
+        for k in range(3):
+            piece = rest.astype(jnp.bfloat16)
+            thirds[k].append(piece)
+            rest = rest - piece.astype(jnp.float32)
+    weight = jnp.concatenate([jnp.concatenate(k, axis=0) for k in thirds], axis=1)
     above_row = lax.broadcasted_iota(jnp.int32, (Z, 2 * Z), 0)
     column = lax.broadcasted_iota(jnp.int32, (Z, 2 * Z), 1)
     triangle = jnp.where(
         (above_row < column) | (column >= Z),
         1.0,
         jnp.where(above_row == column, 0.5, 0.0),
-    ).astype(jnp.float32)
-    sums = jnp.dot(
-        weight, triangle, precision=lax.Precision.HIGHEST, preferred_element_type=jnp.float32
-    )
+    ).astype(jnp.bfloat16)
+    triangle = jnp.concatenate([triangle] * 3, axis=0)
+    sums = jnp.dot(weight, triangle, preferred_element_type=jnp.float32)
     pv[...] = sums[:, :Z] + 1.0
     tot[...] = sums[:, Z:]
     tile = plane
@@ -268,11 +289,9 @@
         xt[i] = tot[pl.ds(at * Y, Y), :]
         yt[i] = tot[pl.ds(line, X, stride=Y), :]
 
-    for copy in loads[2:]:
-        copy.wait()
     tiles = [plane, plane]
 
-    def local(x, tiles):
+    def strain(x):
         base = Y + x * Y
         own = pl.ds(x * Y, Y)
         grad = []
@@ -283,52 +302,58 @@
                 uv[c, pl.ds(base + 1, Y), :] * not_last - uv[c, pl.ds(base - 1, Y), :] * not_first,
                 pltpu.roll(here, Z - 1, 1) * z_last - pltpu.roll(here, 1, 1) * z_first,
             ))
+        el[0, own, :] = grad[0][0]
+        el[1, own, :] = grad[1][1]
+        el[2, own, :] = grad[2][2]
+        el[3, own, :] = 0.5 * (grad[0][1] + grad[1][0])
+        el[4, own, :] = 0.5 * (grad[0][2] + grad[2][0])
+        el[5, own, :] = 0.5 * (grad[1][2] + grad[2][1])
+
+    def pack(k, x, part, tiles):
+        q = (k % 4) * X + x
+        tile = pltpu.roll(part, (2 * q + 1) % Z, 1)
+        tiles[k // 4] = jnp.where(pair == q, tile, tiles[k // 4])
+
+    def factors(x, tiles):
+        own = pl.ds(x * Y, Y)
         minus_two = -2.0 / tv[own, :]
-        parts = [
-            grad[0][0] - ev[0, own, :],
-            grad[1][1] - ev[1, own, :],
-            grad[2][2] - ev[2, own, :],
-            0.5 * (grad[0][1] + grad[1][0]) - ev[3, own, :],
-            0.5 * (grad[0][2] + grad[2][0]) - ev[4, own, :],
-            0.5 * (grad[1][2] + grad[2][1]) - ev[5, own, :],
-            (2.0 + 14.0 * bv[own, :].astype(jnp.float32)) * jnp.exp(pv[own, :] * minus_two),
-            minus_two,
-        ]
-        for k in range(6):
-            el[k, own, :] = parts[k]
-        av[own, :] = parts[6]
-        nt[own, :] = parts[7]
+        factor = (2.0 + 14.0 * bv[own, :].astype(jnp.float32)) * jnp.exp(pv[own, :] * minus_two)
+        av[own, :] = factor
+        nt[own, :] = minus_two
         for i, at in enumerate((0, X - 1)):
             if x == at:
-                for k in range(8):
-                    xs[i, k] = parts[k]
-        tiles = list(tiles)
-        for k in range(8):
-            q = (k % 4) * X + x
-            tile = pltpu.roll(parts[k], (2 * q + 1) % Z, 1)
-            tiles[k // 4] = jnp.where(pair == q, tile, tiles[k // 4])
-        return tiles
+                xs[i, 6] = factor
+                xs[i, 7] = minus_two
+        pack(6, x, factor, tiles)
+        pack(7, x, minus_two, tiles)
+
+    def elastic(x, tiles):
+        own = pl.ds(x * Y, Y)
+        for k in range(6):
+            part = el[k, own, :] - ev[k, own, :]
+            el[k, own, :] = part
+            for i, at in enumerate((0, X - 1)):
+                if x == at:
+                    xs[i, k] = part
+            pack(k, x, part, tiles)
 
     ends = sorted({0, X - 1})
     for x in ends:
-        tiles = local(x, tiles)
-
-    @pl.when(expected > 0)
-    def _():
-        pl.semaphore_wait(barrier, expected)
-
-    for o in lowers:
-        @pl.when(has[o])
-        def _(o=o):
-            pl.semaphore_signal(
-                ready.at[uppers.index(minus(o))], inc=1, device_id=partner(o), device_id_type=MESH
-            )
-    early = ("xu", "xs", "yu", "zu", "xy", "xz", "yz", "t", "tx", "ty")
-    start(lowers, early)
-
-    for x in range(X):
-        if x not in ends:
-            tiles = local(x, tiles)
+        strain(x)
+    for copy in loads[2:6]:
+        copy.wait()
+    for x in ends:
+        elastic(x, tiles)
+        factors(x, tiles)
+    start(lowers, ("xs", "t", "tx", "ty"))
+
+    inner = [x for x in range(X) if x not in ends]
+    for x in inner:
+        strain(x)
+        factors(x, tiles)
+    loads[6].wait()
+    for x in inner:
+        elastic(x, tiles)
     for i, line in enumerate((0, Y - 1)):
         for k in range(8):
             src = el.at[k] if k < 6 else (av, nt)[k - 6]
@@ -342,7 +367,7 @@
         @pl.when(has[o])
         def _(o=o):
             pl.semaphore_wait(ready.at[uppers.index(o)], 1)
-    start(uppers, early + ("ys", "zs"))
+    start(uppers, first + ("xs", "ys", "zs", "t", "tx", "ty"))
 
     arrive("yu")
     for side, line in enumerate((0, Y - 1)):
@@ -564,7 +589,7 @@
             vmem((D, Y, Z), f32),
             vmem((2, D, Y, Z), f32),
             vmem((2, D, X, Z), f32),
-            dma((5,)),
+            dma((7,)),
             pltpu.SemaphoreType.REGULAR((n_upper,)),
         ] + [dma((2,))] * 12 + [dma((2, 2))] * 6 + [dma((D,))] * 2 + [dma((2, D))] * 4,
         compiler_params=pltpu.CompilerParams(collective_id=0, has_side_effects=True),

time: 11.8 us -> 11.7 us (level)
  Pallas kernels: 11.1 us -> 10.9 us
where the time goes in v2:
time: 11.7 us; the launch traced here: 11.6 us
  Pallas kernels  10.9 us (93%)
  between operations  0.64 us (5%)
    pallas_call x1, Pallas kernels, shards(): pl.pallas_call(functools.partial(kernel, (X, Y, Z), sizes), out_shape=(vm...  9.92 us
    pallas_call x1, Pallas kernels, shards(): pl.pallas_call(finish, out_shape=(jax.ShapeDtypeStruct((6, N, Z), f32), j...  1.03 us

profile of v2, /device:TPU:1, one launch (start us, length us, event | category | flops | bytes accessed | tf_op | source)
XLA Modules:
  0.0 11.6 jit_solution(14559430057589637542)
XLA Ops:
  0.6 9.9 %strain_step.1 = (f32[6,256,128]{2,1,0:T(8,128)S(1)}, f32[3,256,128]{2,1,0:T(8,128)S(1)}) custom-call(f32[3,256,128]{2,1,0:T(8,128)} %bitcast.8, f32[6,256,128]{2,1,0:T(8,128)} %bitcast.7, f32[256,128]{1,0:T(8,128)} %bitcast.9, f32[256,128]{1,0:T(8,128)} %bitcast.10, s32[256,128]{1,0:T(8,128)} %bitcast.11), custom_call_target="tpu_custom_call" | custom-call | tf_op jit(solution)/shard_map/strain_step/pallas_call | solution.py:554
  10.6 1.0 %finish.1 = (f32[6,256,128]{2,1,0:T(8,128)}, f32[3,256,128]{2,1,0:T(8,128)}) custom-call(f32[6,256,128]{2,1,0:T(8,128)S(1)} %get-tuple-element.6.fv, f32[3,256,128]{2,1,0:T(8,128)S(1)} %get-tuple-element.7.mv), custom_call_target="tpu_custom_call" | custom-call | tf_op jit(solution)/shard_map/finish/pallas_call | solution.py:598

commit v3 on v2

--- a/solution.py
+++ b/solution.py
@@ -9,7 +9,6 @@
 
 MESH = pl.DeviceIdType.MESH
 AXES = ("gx", "gy", "gz")
-ORDER = (2, 1, 0)
 TERMS = (
     ((0, 0.5), (3, 0.25), (4, 0.25)),
     ((3, 0.25), (1, 0.5), (5, 0.25)),
@@ -18,10 +17,6 @@
 X_SET = (0, 3, 4)
 Y_SET = (3, 1, 5)
 Z_SET = (4, 5, 2)
-
-
-def upper(o):
-    return tuple(o[a] for a in ORDER) > (0, 0, 0)
 
 
 def offsets(layers):
@@ -45,6 +40,22 @@
     return tuple(-v for v in o)
 
 
+def plus(o, p):
+    return tuple(v + w for v, w in zip(o, p))
+
+
+def split(o):
+    return tuple(min(v, 0) for v in o), tuple(max(v, 0) for v in o)
+
+
+def kinds_of(layers):
+    offs = offsets(layers)
+    uppers = [o for o in offs if min(o) >= 0]
+    lowers = [o for o in offs if max(o) <= 0]
+    mixed = [o for o in offs if min(o) < 0 < max(o)]
+    return uppers, lowers, mixed
+
+
 def merge(low, high):
     Z = low.shape[1]
     even = (lax.broadcasted_iota(jnp.int32, low.shape, 1) & 1) == 0
@@ -78,7 +89,7 @@
     uv, ev, tv, rv, bv, pv, tot, el, av, nt, sp,
     xs, ys, yu, zu, zs, xy, zt, xt, yt,
     rxu, rxs, ryu, rys, rzu, rzs, rxy, rxz, ryz, rt, rtx, rty,
-    in_sem, ready,
+    in_sem, ready, told,
     xu_send, xu_recv, xs_send, xs_recv, yu_send, yu_recv, ys_send, ys_recv,
     zu_send, zu_recv, zs_send, zs_recv, xy_send, xy_recv, xz_send, xz_recv, yz_send, yz_recv,
     t_send, t_recv, tx_send, tx_recv, ty_send, ty_recv,
@@ -89,8 +100,7 @@
     depths = range(1, layers)
     me = [lax.axis_index(a) for a in AXES]
     offs = offsets(layers)
-    uppers = [o for o in offs if upper(o)]
-    lowers = [o for o in offs if not upper(o)]
+    uppers, lowers, mixed = kinds_of(layers)
 
     def exists(o):
         ok = None
@@ -225,6 +235,17 @@
                 def _(copy=copy):
                     copy.wait_recv()
 
+    @pl.when(expected > 0)
+    def _():
+        pl.semaphore_wait(barrier, expected)
+
+    for o in lowers:
+        @pl.when(has[o])
+        def _(o=o):
+            pl.semaphore_signal(
+                ready.at[uppers.index(minus(o))], inc=1, device_id=partner(o), device_id_type=MESH
+            )
+
     loads[0].wait()
     tile0 = plane
     for x in range(X):
@@ -245,16 +266,6 @@
                 xy[j, i, pl.ds(c, 1), :] = uv[c, pl.ds(Y + at * Y + line, 1), :]
     zu[1, pl.ds(0, X), :] = tile
 
-    @pl.when(expected > 0)
-    def _():
-        pl.semaphore_wait(barrier, expected)
-
-    for o in lowers:
-        @pl.when(has[o])
-        def _(o=o):
-            pl.semaphore_signal(
-                ready.at[uppers.index(minus(o))], inc=1, device_id=partner(o), device_id_type=MESH
-            )
     first = ("xu", "yu", "zu", "xy", "xz", "yz")
     start(lowers, first)
 
@@ -363,11 +374,27 @@
         zs[k] = tiles[k]
     start(lowers, ("zs",))
 
-    for o in uppers:
+    everything = first + ("xs", "ys", "zs", "t", "tx", "ty")
+    for o in sorted(uppers, key=lambda o: sum(map(abs, o))):
         @pl.when(has[o])
         def _(o=o):
             pl.semaphore_wait(ready.at[uppers.index(o)], 1)
-    start(uppers, first + ("xs", "ys", "zs", "t", "tx", "ty"))
+
+        start([o], everything)
+    for o in mixed:
+        low, high = split(o)
+
+        @pl.when(jnp.logical_and(has[minus(low)], has[high]))
+        def _(o=o, low=low):
+            pl.semaphore_signal(
+                told.at[mixed.index(o)], inc=1, device_id=partner(minus(low)), device_id_type=MESH
+            )
+    for o in mixed:
+        @pl.when(has[o])
+        def _(o=o):
+            pl.semaphore_wait(told.at[mixed.index(o)], 1)
+
+        start([o], everything)
 
     arrive("yu")
     for side, line in enumerate((0, Y - 1)):
@@ -550,7 +577,7 @@
     any_space = pl.BlockSpec(memory_space=pl.ANY)
     in_vmem = pl.BlockSpec(memory_space=vmem)
     D = max(layers - 1, 1)
-    n_upper = sum(upper(o) for o in offsets(layers))
+    uppers, _, mixed = kinds_of(layers)
     kept = pl.pallas_call(
         functools.partial(kernel, (X, Y, Z), sizes),
         out_shape=(vmem((6, N, Z), f32), vmem((3, N, Z), f32)),
@@ -590,7 +617,8 @@
             vmem((2, D, Y, Z), f32),
             vmem((2, D, X, Z), f32),
             dma((7,)),
-            pltpu.SemaphoreType.REGULAR((n_upper,)),
+            pltpu.SemaphoreType.REGULAR((len(uppers),)),
+            pltpu.SemaphoreType.REGULAR((len(mixed),)),
         ] + [dma((2,))] * 12 + [dma((2, 2))] * 6 + [dma((D,))] * 2 + [dma((2, D))] * 4,
         compiler_params=pltpu.CompilerParams(collective_id=0, has_side_effects=True),
         name="strain_step",

time: 11.7 us -> 11.2 us (0.957)
  Pallas kernels: 10.9 us -> 10.4 us
    pallas_call x1, Pallas kernels: 9.92 us -> 9.39 us  [shards(): pl.pallas_call(functools.partial(kernel, (X, Y, Z), sizes), out_shape=(vm...]
where the time goes in v3:
time: 11.2 us; the launch traced here: 11.1 us
  Pallas kernels  10.4 us (93%)
  between operations  0.64 us (6%)
    pallas_call x1, Pallas kernels, shards(): pl.pallas_call(functools.partial(kernel, (X, Y, Z), sizes), out_shape=(vm...  9.39 us
    pallas_call x1, Pallas kernels, shards(): pl.pallas_call(finish, out_shape=(jax.ShapeDtypeStruct((6, N, Z), f32), j...  1.03 us

profile of v3, /device:TPU:1, one launch (start us, length us, event | category | flops | bytes accessed | tf_op | source)
XLA Modules:
  0.0 11.1 jit_solution(3489777374998075121)
XLA Ops:
  0.6 9.4 %strain_step.1 = (f32[6,256,128]{2,1,0:T(8,128)S(1)}, f32[3,256,128]{2,1,0:T(8,128)S(1)}) custom-call(f32[3,256,128]{2,1,0:T(8,128)} %bitcast.8, f32[6,256,128]{2,1,0:T(8,128)} %bitcast.7, f32[256,128]{1,0:T(8,128)} %bitcast.9, f32[256,128]{1,0:T(8,128)} %bitcast.10, s32[256,128]{1,0:T(8,128)} %bitcast.11), custom_call_target="tpu_custom_call" | custom-call | tf_op jit(solution)/shard_map/strain_step/pallas_call | solution.py:581
  10.0 1.0 %finish.1 = (f32[6,256,128]{2,1,0:T(8,128)}, f32[3,256,128]{2,1,0:T(8,128)}) custom-call(f32[6,256,128]{2,1,0:T(8,128)S(1)} %get-tuple-element.6.fv, f32[3,256,128]{2,1,0:T(8,128)S(1)} %get-tuple-element.7.mv), custom_call_target="tpu_custom_call" | custom-call | tf_op jit(solution)/shard_map/finish/pallas_call | solution.py:626

commit v4 on v3

--- a/solution.py
+++ b/solution.py
@@ -89,10 +89,7 @@
     uv, ev, tv, rv, bv, pv, tot, el, av, nt, sp,
     xs, ys, yu, zu, zs, xy, zt, xt, yt,
     rxu, rxs, ryu, rys, rzu, rzs, rxy, rxz, ryz, rt, rtx, rty,
-    in_sem, ready, told,
-    xu_send, xu_recv, xs_send, xs_recv, yu_send, yu_recv, ys_send, ys_recv,
-    zu_send, zu_recv, zs_send, zs_recv, xy_send, xy_recv, xz_send, xz_recv, yz_send, yz_recv,
-    t_send, t_recv, tx_send, tx_recv, ty_send, ty_recv,
+    in_sem, ready, told, send_sem, recv_sem,
 ):
     X, Y, Z = dims
     N = X * Y
@@ -101,6 +98,10 @@
     me = [lax.axis_index(a) for a in AXES]
     offs = offsets(layers)
     uppers, lowers, mixed = kinds_of(layers)
+    W = max(X, Y)
+
+    def ready_index(o):
+        return o.index(1) if sum(o) == 1 else 3
 
     def exists(o):
         ok = None
@@ -118,7 +119,7 @@
     faces = {a: [tuple(s if i == a else 0 for i in range(3)) for s in (-1, 1)] for a in range(3)}
 
     loads = [
-        pltpu.make_async_copy(src, dst, in_sem.at[i])
+        pltpu.make_async_copy(src, dst, in_sem.at[min(i, 2) if i < 6 else 3])
         for i, (src, dst) in enumerate(
             (
                 (u_hbm, uv.at[:, pl.ds(Y, N), :]),
@@ -133,6 +134,11 @@
     ]
     for copy in loads:
         copy.start()
+
+    def take(sem, rows):
+        planes = next(k for k in range(1, 7) if rows % (8 * k) == 0 and rows // k <= N + 2 * Y)
+        spot = sp.at[pl.ds(0, planes), pl.ds(0, rows // planes)]
+        pltpu.make_async_copy(spot, spot, sem).wait()
 
     barrier = pltpu.get_barrier_semaphore()
     for o in uppers:
@@ -188,36 +194,60 @@
         row_x = lax.broadcasted_iota(jnp.int32, (X, Z), 0)
         z_edge_x = jnp.where(lane_x == 0, -0.5, jnp.where(lane_x == Z - 1, 0.5, 0.0)).astype(jnp.float32)
 
+    beside = [sum(has[o].astype(jnp.int32) for o in faces[a]) for a in range(3)]
+    some = [1, 2]
+    above, below = me[2], layers - 1 - me[2]
+    counts = {
+        "xu": (3 * Y, beside[0], some), "xs": (8 * Y, beside[0], some),
+        "yu": (3 * X, beside[1], some), "ys": (8 * X, beside[1], some),
+        "zu": (Y, beside[2], some), "zs": (2 * Y, beside[2], some),
+        "xy": (8, beside[0] * beside[1], [1, 2, 4]),
+        "xz": (Y, beside[0] * beside[2], [1, 2, 4]),
+        "yz": (2 * W, beside[1] * beside[2], [1, 2, 4]),
+    }
+    totals = {
+        "t": (Y, 1, list(depths)),
+        "tx": (Y, beside[0], sorted({n * d for n in some for d in depths})),
+        "ty": (X, beside[1], sorted({n * d for n in some for d in depths})),
+    }
+    recv_index = {kind: i for i, kind in enumerate((*counts, *totals))}
+    send_index = {
+        "xu": 0, "xs": 0, "yu": 1, "ys": 1, "zu": 2, "zs": 2, "xy": 3, "xz": 4, "yz": 5, "t": 6, "tx": 7, "ty": 8,
+    }
     sends = {o: [] for o in offs}
-    recvs = {}
-
-    def message(kind, o, src, dst, send, recv):
-        copy = pltpu.make_async_remote_copy(
-            src_ref=src, dst_ref=dst, send_sem=send, recv_sem=recv,
+
+    def message(kind, o, src, dst):
+        sends[o].append((kind, pltpu.make_async_remote_copy(
+            src_ref=src, dst_ref=dst,
+            send_sem=send_sem.at[send_index[kind]], recv_sem=recv_sem.at[recv_index[kind]],
             device_id=partner(o), device_id_type=MESH,
-        )
-        sends[o].append((kind, copy))
-        recvs[kind, minus(o)] = copy
+        )))
 
     for i, s in enumerate((-1, 1)):
         k = 1 - i
         at = (Y, Y * X)[i]
-        message("xu", (s, 0, 0), uv.at[:, pl.ds(at, Y), :], rxu.at[k], xu_send.at[i], xu_recv.at[k])
-        message("xs", (s, 0, 0), xs.at[i], rxs.at[k], xs_send.at[i], xs_recv.at[k])
-        message("yu", (0, s, 0), yu.at[i], ryu.at[k], yu_send.at[i], yu_recv.at[k])
-        message("ys", (0, s, 0), ys.at[i], rys.at[k], ys_send.at[i], ys_recv.at[k])
-        message("zu", (0, 0, s), zu.at[0, pl.ds(0, Y)], rzu.at[k], zu_send.at[i], zu_recv.at[k])
-        message("zs", (0, 0, s), zs, rzs.at[k], zs_send.at[i], zs_recv.at[k])
+        message("xu", (s, 0, 0), uv.at[:, pl.ds(at, Y), :], rxu.at[k])
+        message("xs", (s, 0, 0), xs.at[i], rxs.at[k])
+        message("yu", (0, s, 0), yu.at[i], ryu.at[k])
+        message("ys", (0, s, 0), ys.at[i], rys.at[k])
+        message("zu", (0, 0, s), zu.at[0, pl.ds(0, Y)], rzu.at[k])
+        message("zs", (0, 0, s), zs, rzs.at[k])
         for j, s2 in enumerate((-1, 1)):
             m = 1 - j
-            message("xy", (s, s2, 0), xy.at[i, j], rxy.at[k, m], xy_send.at[i, j], xy_recv.at[k, m])
-            message("xz", (s, 0, s2), zu.at[0, pl.ds(0, Y)], rxz.at[k, m], xz_send.at[i, j], xz_recv.at[k, m])
-            message("yz", (0, s, s2), zu, ryz.at[k, m], yz_send.at[i, j], yz_recv.at[k, m])
+            message("xy", (s, s2, 0), xy.at[i, j], rxy.at[k, m])
+            message("xz", (s, 0, s2), zu.at[0, pl.ds(0, Y)], rxz.at[k, m])
+            message("yz", (0, s, s2), zu, ryz.at[k, m])
         for d in depths:
-            message("tx", (s, 0, d), xt.at[i], rtx.at[k, d - 1], tx_send.at[i, d - 1], tx_recv.at[k, d - 1])
-            message("ty", (0, s, d), yt.at[i], rty.at[k, d - 1], ty_send.at[i, d - 1], ty_recv.at[k, d - 1])
+            message("tx", (s, 0, d), xt.at[i], rtx.at[k, d - 1])
+            message("ty", (0, s, d), yt.at[i], rty.at[k, d - 1])
     for d in depths:
-        message("t", (0, 0, d), zt, rt.at[d - 1], t_send.at[d - 1], t_recv.at[d - 1])
+        message("t", (0, 0, d), zt, rt.at[d - 1])
+
+    def settle(sem, rows, count, values):
+        for n in values:
+            @pl.when(count == n)
+            def _(n=n):
+                take(sem, n * rows)
 
     def start(offsets_in, kinds):
         for o in offsets_in:
@@ -229,11 +259,13 @@
                         copy.start()
 
     def arrive(*kinds):
-        for (kind, o), copy in recvs.items():
-            if kind in kinds:
-                @pl.when(has[o])
-                def _(copy=copy):
-                    copy.wait_recv()
+        for kind in kinds:
+            if kind in counts:
+                rows, count, values = counts[kind]
+            else:
+                rows, count, values = totals[kind]
+                count = count * above
+            settle(recv_sem.at[recv_index[kind]], rows, count, values)
 
     @pl.when(expected > 0)
     def _():
@@ -243,8 +275,17 @@
         @pl.when(has[o])
         def _(o=o):
             pl.semaphore_signal(
-                ready.at[uppers.index(minus(o))], inc=1, device_id=partner(o), device_id_type=MESH
+                ready.at[ready_index(minus(o))], inc=1, device_id=partner(o), device_id_type=MESH
             )
+
+    def announce(o):
+        low, high = split(o)
+
+        @pl.when(jnp.logical_and(has[minus(low)], has[high]))
+        def _():
+            pl.semaphore_signal(told.at[0], inc=1, device_id=partner(minus(low)), device_id_type=MESH)
+
+    lowers = sorted(lowers, key=lambda o: (sum(map(abs, o)), o[2], o[1]))
 
     loads[0].wait()
     tile0 = plane
@@ -351,8 +392,7 @@
     ends = sorted({0, X - 1})
     for x in ends:
         strain(x)
-    for copy in loads[2:6]:
-        copy.wait()
+    take(in_sem.at[2], 12 * Y + 2 * N)
     for x in ends:
         elastic(x, tiles)
         factors(x, tiles)
@@ -375,26 +415,36 @@
     start(lowers, ("zs",))
 
     everything = first + ("xs", "ys", "zs", "t", "tx", "ty")
-    for o in sorted(uppers, key=lambda o: sum(map(abs, o))):
+    near = [o for o in uppers if sum(o) == 1]
+    for o in sorted(near):
         @pl.when(has[o])
         def _(o=o):
-            pl.semaphore_wait(ready.at[uppers.index(o)], 1)
-
-        start([o], everything)
+            pl.semaphore_wait(ready.at[ready_index(o)], 1)
+
     for o in mixed:
         low, high = split(o)
-
-        @pl.when(jnp.logical_and(has[minus(low)], has[high]))
-        def _(o=o, low=low):
-            pl.semaphore_signal(
-                told.at[mixed.index(o)], inc=1, device_id=partner(minus(low)), device_id_type=MESH
-            )
+        if high in near and minus(low) in near:
+            announce(o)
+    start(sorted(near), everything)
+    others = [o for o in uppers if o not in near]
+    total = sum(has[o].astype(jnp.int32) for o in others)
+
+    @pl.when(total > 0)
+    def _():
+        pl.semaphore_wait(ready.at[3], total)
+
     for o in mixed:
-        @pl.when(has[o])
-        def _(o=o):
-            pl.semaphore_wait(told.at[mixed.index(o)], 1)
-
-        start([o], everything)
+        low, high = split(o)
+        if not (high in near and minus(low) in near):
+            announce(o)
+    start(others, everything)
+    total_mixed = sum(has[o].astype(jnp.int32) for o in mixed)
+
+    @pl.when(total_mixed > 0)
+    def _():
+        pl.semaphore_wait(told.at[0], total_mixed)
+
+    start(mixed, everything)
 
     arrive("yu")
     for side, line in enumerate((0, Y - 1)):
@@ -461,24 +511,36 @@
     def ends_of(first, last, rows, count):
         return jnp.where(rows == 0, -first, jnp.where(rows == count - 1, last, 0.0))
 
-    arrive("ys", "xy", "yz", "ty")
-    for side, line in enumerate((0, Y - 1)):
-        @pl.when(has[faces[1][side]])
-        def _(side=side, line=line):
-            e = [rys[side, k] for k in range(6)]
-            add(e, 1, 1.0 - 2.0 * side, [uv[c, pl.ds(Y + line, X, stride=Y), :] for c in range(3)])
-            add(e, 0, 1.0, [
-                ends_of(rxy[0, side, pl.ds(c, 1), :], rxy[1, side, pl.ds(c, 1), :], row_x, X) for c in range(3)
-            ])
-            joined = merge(ryz[side, 0, 1, pl.ds(0, X), :], ryz[side, 1, 1, pl.ds(0, X), :])
-            add(e, 2, 2.0, [edge_term(joined, 3 * (1 - side) + c, z_edge_x) for c in range(3)])
-            load = row_plane
-            for d in depths:
-                load = load + rty[side, d - 1]
-            trace, change = flow(e, rys[side, 6] * jnp.exp(load * rys[side, 7]))
-            own = pl.ds(line, X, stride=Y)
-            for c in range(3):
-                mv[c, own, :] = mv[c, own, :] + (side - 0.5) * stress(e, change, trace, Y_SET[c])
+    def along_gy():
+        arrive("ys", "ty")
+        for side, line in enumerate((0, Y - 1)):
+            @pl.when(has[faces[1][side]])
+            def _(side=side, line=line):
+                e = [rys[side, k] for k in range(6)]
+                add(e, 1, 1.0 - 2.0 * side, [uv[c, pl.ds(Y + line, X, stride=Y), :] for c in range(3)])
+                add(e, 0, 1.0, [
+                    ends_of(rxy[0, side, pl.ds(c, 1), :], rxy[1, side, pl.ds(c, 1), :], row_x, X) for c in range(3)
+                ])
+                joined = merge(ryz[side, 0, 1, pl.ds(0, X), :], ryz[side, 1, 1, pl.ds(0, X), :])
+                add(e, 2, 2.0, [edge_term(joined, 3 * (1 - side) + c, z_edge_x) for c in range(3)])
+                load = row_plane
+                for d in depths:
+                    load = load + rty[side, d - 1]
+                trace, change = flow(e, rys[side, 6] * jnp.exp(load * rys[side, 7]))
+                own = pl.ds(line, X, stride=Y)
+                for c in range(3):
+                    mv[c, own, :] = mv[c, own, :] + (side - 0.5) * stress(e, change, trace, Y_SET[c])
+
+    first_row = me[1] == 0
+
+    @pl.when(first_row)
+    def _():
+        arrive("xy", "yz")
+        along_gy()
+
+    @pl.when(jnp.logical_not(first_row))
+    def _():
+        arrive("yz")
 
     arrive("zs", "xz")
     block = 2 * X
@@ -526,6 +588,10 @@
             own = pl.ds(x * Y, Y)
             mv[c, own, :] = mv[c, own, :] + edge_term(joined, c * X + x, z_edge)
 
+    @pl.when(jnp.logical_not(first_row))
+    def _():
+        arrive("xy")
+
     arrive("xs", "tx")
     for side, at in enumerate((0, X - 1)):
         @pl.when(has[faces[0][side]])
@@ -546,12 +612,14 @@
             for c in range(3):
                 mv[c, own, :] = mv[c, own, :] + (side - 0.5) * stress(e, change, trace, X_SET[c])
 
-    for o in offs:
-        if sends[o]:
-            @pl.when(has[o])
-            def _(o=o):
-                for _, copy in sends[o]:
-                    copy.wait_send()
+    pl.when(jnp.logical_not(first_row))(along_gy)
+    settle(send_sem.at[0], 11 * Y, beside[0], some)
+    settle(send_sem.at[1], 11 * X, beside[1], some)
+    settle(send_sem.at[2], 3 * Y, beside[2], some)
+    for i, kind in enumerate(("xy", "xz", "yz")):
+        settle(send_sem.at[3 + i], *counts[kind])
+    for i, (rows, count, values) in enumerate(totals.values()):
+        settle(send_sem.at[6 + i], rows, count * below, values)
 
 
 def finish(fv, mv, f_hbm, m_hbm, sem):
@@ -577,7 +645,6 @@
     any_space = pl.BlockSpec(memory_space=pl.ANY)
     in_vmem = pl.BlockSpec(memory_space=vmem)
     D = max(layers - 1, 1)
-    uppers, _, mixed = kinds_of(layers)
     kept = pl.pallas_call(
         functools.partial(kernel, (X, Y, Z), sizes),
         out_shape=(vmem((6, N, Z), f32), vmem((3, N, Z), f32)),
@@ -616,10 +683,12 @@
             vmem((D, Y, Z), f32),
             vmem((2, D, Y, Z), f32),
             vmem((2, D, X, Z), f32),
-            dma((7,)),
-            pltpu.SemaphoreType.REGULAR((len(uppers),)),
-            pltpu.SemaphoreType.REGULAR((len(mixed),)),
-        ] + [dma((2,))] * 12 + [dma((2, 2))] * 6 + [dma((D,))] * 2 + [dma((2, D))] * 4,
+            dma((4,)),
+            pltpu.SemaphoreType.REGULAR((4,)),
+            pltpu.SemaphoreType.REGULAR((1,)),
+            dma((9,)),
+            dma((12,)),
+        ],
         compiler_params=pltpu.CompilerParams(collective_id=0, has_side_effects=True),
         name="strain_step",
     )(u.reshape(3, N, Z), e.reshape(6, N, Z), t.reshape(N, Z), r.reshape(N, Z), b.reshape(N, Z))

time: 11.2 us -> 10.3 us (0.920)
  the two profiles are of different devices: /device:TPU:1 before, /device:TPU:19 now
where the time goes in v4:
time: 10.3 us; the launch traced here: 10.1 us
  Pallas kernels  9.47 us (92%)
  between operations  0.64 us (6%)
    pallas_call x1, Pallas kernels, shards(): pl.pallas_call(functools.partial(kernel, (X, Y, Z), sizes), out_shape=(vm...  8.44 us
    pallas_call x1, Pallas kernels, shards(): pl.pallas_call(finish, out_shape=(jax.ShapeDtypeStruct((6, N, Z), f32), j...  1.03 us

profile of v4, /device:TPU:19, one launch (start us, length us, event | category | flops | bytes accessed | tf_op | source)
XLA Modules:
  0.0 10.1 jit_solution(4213842419978119825)
XLA Ops:
  0.6 8.4 %strain_step.1 = (f32[6,256,128]{2,1,0:T(8,128)S(1)}, f32[3,256,128]{2,1,0:T(8,128)S(1)}) custom-call(f32[3,256,128]{2,1,0:T(8,128)} %bitcast.8, f32[6,256,128]{2,1,0:T(8,128)} %bitcast.7, f32[256,128]{1,0:T(8,128)} %bitcast.9, f32[256,128]{1,0:T(8,128)} %bitcast.10, s32[256,128]{1,0:T(8,128)} %bitcast.11), custom_call_target="tpu_custom_call" | custom-call | tf_op jit(solution)/shard_map/strain_step/pallas_call | solution.py:648
  9.1 1.0 %finish.1 = (f32[6,256,128]{2,1,0:T(8,128)}, f32[3,256,128]{2,1,0:T(8,128)}) custom-call(f32[6,256,128]{2,1,0:T(8,128)S(1)} %get-tuple-element.6.fv, f32[3,256,128]{2,1,0:T(8,128)S(1)} %get-tuple-element.7.mv), custom_call_target="tpu_custom_call" | custom-call | tf_op jit(solution)/shard_map/finish/pallas_call | solution.py:695

commit v5 on v4

--- a/solution.py
+++ b/solution.py
@@ -84,7 +84,7 @@
 
 def kernel(
     dims, sizes,
-    u_hbm, e_hbm, t_hbm, r_hbm, b_hbm,
+    u_hbm, u_rows, e_hbm, t_hbm, r_hbm, b_hbm,
     fv, mv,
     uv, ev, tv, rv, bv, pv, tot, el, av, nt, sp,
     xs, ys, yu, zu, zs, xy, zt, xt, yt,
@@ -195,24 +195,37 @@
         z_edge_x = jnp.where(lane_x == 0, -0.5, jnp.where(lane_x == Z - 1, 0.5, 0.0)).astype(jnp.float32)
 
     beside = [sum(has[o].astype(jnp.int32) for o in faces[a]) for a in range(3)]
-    some = [1, 2]
     above, below = me[2], layers - 1 - me[2]
-    counts = {
-        "xu": (3 * Y, beside[0], some), "xs": (8 * Y, beside[0], some),
-        "yu": (3 * X, beside[1], some), "ys": (8 * X, beside[1], some),
-        "zu": (Y, beside[2], some), "zs": (2 * Y, beside[2], some),
-        "xy": (8, beside[0] * beside[1], [1, 2, 4]),
-        "xz": (Y, beside[0] * beside[2], [1, 2, 4]),
-        "yz": (2 * W, beside[1] * beside[2], [1, 2, 4]),
+
+    def products(*ranges):
+        values = {1}
+        for r in ranges:
+            values = {v * w for v in values for w in r}
+        return sorted(values - {0})
+
+    some, any_depth = (1, 2), range(layers)
+    four = products(some, some)
+    arrivals = {
+        "xu": (3 * Y, beside[0], some),
+        "xs": (Y, beside[0] * (8 + above), products(some, [8 + d for d in any_depth])),
+        "yu": (3 * X, beside[1], some),
+        "ys": (X, beside[1] * (8 + above), products(some, [8 + d for d in any_depth])),
+        "zu": (Y, beside[2] + above, sorted({n + d for n in some for d in any_depth})),
+        "zs": (2 * Y, beside[2], some),
+        "xy": (8, beside[0] * beside[1], four),
+        "xz": (3 * Y, beside[0] * beside[2], four),
+        "yz": (2 * W, beside[1] * beside[2], four),
     }
-    totals = {
-        "t": (Y, 1, list(depths)),
-        "tx": (Y, beside[0], sorted({n * d for n in some for d in depths})),
-        "ty": (X, beside[1], sorted({n * d for n in some for d in depths})),
-    }
-    recv_index = {kind: i for i, kind in enumerate((*counts, *totals))}
+    departures = (
+        (Y, beside[0] * (11 + below), products(some, [11 + d for d in any_depth])),
+        (X, beside[1] * (11 + below), products(some, [11 + d for d in any_depth])),
+        (Y, 3 * beside[2] + below, sorted({3 * n + d for n in some for d in any_depth})),
+        arrivals["xy"], arrivals["xz"], arrivals["yz"],
+    )
+    recv_index = {kind: i for i, kind in enumerate(arrivals)}
+    recv_index |= {"tx": recv_index["xs"], "ty": recv_index["ys"], "t": recv_index["zu"]}
     send_index = {
-        "xu": 0, "xs": 0, "yu": 1, "ys": 1, "zu": 2, "zs": 2, "xy": 3, "xz": 4, "yz": 5, "t": 6, "tx": 7, "ty": 8,
+        "xu": 0, "xs": 0, "tx": 0, "yu": 1, "ys": 1, "ty": 1, "zu": 2, "zs": 2, "t": 2, "xy": 3, "xz": 4, "yz": 5,
     }
     sends = {o: [] for o in offs}
 
@@ -226,16 +239,18 @@
     for i, s in enumerate((-1, 1)):
         k = 1 - i
         at = (Y, Y * X)[i]
-        message("xu", (s, 0, 0), uv.at[:, pl.ds(at, Y), :], rxu.at[k])
+        strike = u_hbm.at[:, pl.ds((0, N - Y)[i], Y), :] if s < 0 else uv.at[:, pl.ds(at, Y), :]
+        message("xu", (s, 0, 0), strike, rxu.at[k])
         message("xs", (s, 0, 0), xs.at[i], rxs.at[k])
-        message("yu", (0, s, 0), yu.at[i], ryu.at[k])
+        message("yu", (0, s, 0), u_rows.at[:, :, 0, :] if s < 0 else yu, ryu.at[k])
         message("ys", (0, s, 0), ys.at[i], rys.at[k])
         message("zu", (0, 0, s), zu.at[0, pl.ds(0, Y)], rzu.at[k])
         message("zs", (0, 0, s), zs, rzs.at[k])
         for j, s2 in enumerate((-1, 1)):
             m = 1 - j
             message("xy", (s, s2, 0), xy.at[i, j], rxy.at[k, m])
-            message("xz", (s, 0, s2), zu.at[0, pl.ds(0, Y)], rxz.at[k, m])
+            strike = u_hbm.at[:, pl.ds(0, Y), :] if s + s2 < 0 else uv.at[:, pl.ds(at, Y), :]
+            message("xz", (s, 0, s2), strike, rxz.at[k, m])
             message("yz", (0, s, s2), zu, ryz.at[k, m])
         for d in depths:
             message("tx", (s, 0, d), xt.at[i], rtx.at[k, d - 1])
@@ -260,12 +275,7 @@
 
     def arrive(*kinds):
         for kind in kinds:
-            if kind in counts:
-                rows, count, values = counts[kind]
-            else:
-                rows, count, values = totals[kind]
-                count = count * above
-            settle(recv_sem.at[recv_index[kind]], rows, count, values)
+            settle(recv_sem.at[recv_index[kind]], *arrivals[kind])
 
     @pl.when(expected > 0)
     def _():
@@ -283,9 +293,12 @@
 
         @pl.when(jnp.logical_and(has[minus(low)], has[high]))
         def _():
-            pl.semaphore_signal(told.at[0], inc=1, device_id=partner(minus(low)), device_id_type=MESH)
+            kind = 0 if max(high) == 1 and min(low) == -1 else 1
+            pl.semaphore_signal(told.at[kind], inc=1, device_id=partner(minus(low)), device_id_type=MESH)
 
     lowers = sorted(lowers, key=lambda o: (sum(map(abs, o)), o[2], o[1]))
+    for kind in ("xz", "yu", "xu"):
+        start(lowers, (kind,))
 
     loads[0].wait()
     tile0 = plane
@@ -295,20 +308,21 @@
             tile = pltpu.roll(uv[c, pl.ds(Y + x * Y, Y), :], (2 * q + 1) % Z, 1)
             tile0 = jnp.where(pair == q, tile, tile0)
     zu[0, pl.ds(0, Y), :] = tile0
+    start(lowers, ("zu",))
     tile = row_plane
     pair_x = lax.broadcasted_iota(jnp.int32, (X, Z), 1) >> 1
     for i, line in enumerate((0, Y - 1)):
         for c in range(3):
             p = 3 * i + c
             lines = uv[c, pl.ds(Y + line, X, stride=Y), :]
-            yu[i, c] = lines
+            if i:
+                yu[c] = lines
             tile = jnp.where(pair_x == p, pltpu.roll(lines, (2 * p + 1) % Z, 1), tile)
             for j, at in enumerate((0, X - 1)):
                 xy[j, i, pl.ds(c, 1), :] = uv[c, pl.ds(Y + at * Y + line, 1), :]
     zu[1, pl.ds(0, X), :] = tile
 
-    first = ("xu", "yu", "zu", "xy", "xz", "yz")
-    start(lowers, first)
+    start(lowers, ("xy", "yz"))
 
     loads[1].wait()
     total_depth = Z * layers
@@ -414,7 +428,7 @@
         zs[k] = tiles[k]
     start(lowers, ("zs",))
 
-    everything = first + ("xs", "ys", "zs", "t", "tx", "ty")
+    everything = ("zu", "yu", "xu", "t", "zs", "ys", "xs", "tx", "ty", "xy", "xz", "yz")
     near = [o for o in uppers if sum(o) == 1]
     for o in sorted(near):
         @pl.when(has[o])
@@ -427,24 +441,24 @@
             announce(o)
     start(sorted(near), everything)
     others = [o for o in uppers if o not in near]
-    total = sum(has[o].astype(jnp.int32) for o in others)
-
-    @pl.when(total > 0)
-    def _():
-        pl.semaphore_wait(ready.at[3], total)
-
-    for o in mixed:
-        low, high = split(o)
-        if not (high in near and minus(low) in near):
-            announce(o)
-    start(others, everything)
-    total_mixed = sum(has[o].astype(jnp.int32) for o in mixed)
-
-    @pl.when(total_mixed > 0)
-    def _():
-        pl.semaphore_wait(told.at[0], total_mixed)
-
-    start(mixed, everything)
+    far = [o for o in mixed if split(o)[1] not in near or minus(split(o)[0]) not in near]
+    close = [o for o in mixed if o not in far]
+
+    def hear(offsets_in, sem):
+        number = sum(has[o].astype(jnp.int32) for o in offsets_in)
+
+        @pl.when(number > 0)
+        def _():
+            pl.semaphore_wait(sem, number)
+
+        start(offsets_in, everything)
+
+    hear(close, told.at[0])
+    hear(others, ready.at[3])
+    for o in far:
+        announce(o)
+    if far:
+        hear(far, told.at[1])
 
     arrive("yu")
     for side, line in enumerate((0, Y - 1)):
@@ -456,7 +470,7 @@
             for c, (part, factor) in enumerate(TERMS[1]):
                 el[part, own, :] = el[part, own, :] + (sign * factor) * ryu[side, c]
 
-    arrive("zu", "t")
+    arrive("zu")
     carried = plane
     for d in depths:
         carried = carried + rt[d - 1]
@@ -512,7 +526,7 @@
         return jnp.where(rows == 0, -first, jnp.where(rows == count - 1, last, 0.0))
 
     def along_gy():
-        arrive("ys", "ty")
+        arrive("ys")
         for side, line in enumerate((0, Y - 1)):
             @pl.when(has[faces[1][side]])
             def _(side=side, line=line):
@@ -552,12 +566,12 @@
     parts = [shift(halo[k // 4], -(k % 4) * block) for k in range(8)]
     mine = zu[0, pl.ds(0, Y), :]
     from_z = jnp.where(even, shift(mine, -1), -shift(mine, 1))
-    left = jnp.where(even, rxz[0, 0], rxz[0, 1])
-    right = jnp.where(even, rxz[1, 0], rxz[1, 1])
-    spot = pair % X
-    from_x = jnp.where(
-        spot == 0, -shift(left, -2 * (X - 1)), jnp.where(spot == X - 1, shift(right, 2 * (X - 1)), 0.0)
-    )
+    from_x = []
+    for c in range(3):
+        left, right = (jnp.where(lane == Z - 1, rxz[i, 0, c], rxz[i, 1, c]) for i in range(2))
+        from_x.append(jnp.where(
+            pair == 0, -shift(left, 1), jnp.where(pair == X - 1, shift(right, 2 * X - 1), 0.0)
+        ))
     even_row = (lax.broadcasted_iota(jnp.int32, (1, Z), 1) & 1) == 0
     from_y = ends_of(
         jnp.where(even_row, ryz[0, 0, 0, pl.ds(Y - 1, 1), :], ryz[0, 1, 0, pl.ds(Y - 1, 1), :]),
@@ -565,7 +579,8 @@
         row, Y,
     )
     e = list(parts[:6])
-    for axis, tile in enumerate((from_x, from_y, from_z)):
+    add(e, 0, 1.0, from_x)
+    for axis, tile in ((1, from_y), (2, from_z)):
         add(e, axis, 1.0, [shift(tile, -c * block) for c in range(3)])
     deeper = plane
     for d in depths:
@@ -592,7 +607,7 @@
     def _():
         arrive("xy")
 
-    arrive("xs", "tx")
+    arrive("xs")
     for side, at in enumerate((0, X - 1)):
         @pl.when(has[faces[0][side]])
         def _(side=side, at=at):
@@ -601,9 +616,13 @@
             add(e, 1, 1.0, [
                 ends_of(rxy[side, 0, pl.ds(c, 1), :], rxy[side, 1, pl.ds(c, 1), :], row, Y) for c in range(3)
             ])
-            facing = (X - 1) * (1 - side)
-            joined = merge(rxz[side, 0], rxz[side, 1])
-            add(e, 2, 2.0, [edge_term(joined, c * X + facing, z_edge) for c in range(3)])
+            add(e, 2, 1.0, [
+                jnp.where(
+                    lane == 0, -pltpu.roll(rxz[side, 0, c], 1, 1),
+                    jnp.where(lane == Z - 1, pltpu.roll(rxz[side, 1, c], Z - 1, 1), 0.0),
+                )
+                for c in range(3)
+            ])
             load = plane
             for d in depths:
                 load = load + rtx[side, d - 1]
@@ -613,13 +632,8 @@
                 mv[c, own, :] = mv[c, own, :] + (side - 0.5) * stress(e, change, trace, X_SET[c])
 
     pl.when(jnp.logical_not(first_row))(along_gy)
-    settle(send_sem.at[0], 11 * Y, beside[0], some)
-    settle(send_sem.at[1], 11 * X, beside[1], some)
-    settle(send_sem.at[2], 3 * Y, beside[2], some)
-    for i, kind in enumerate(("xy", "xz", "yz")):
-        settle(send_sem.at[3 + i], *counts[kind])
-    for i, (rows, count, values) in enumerate(totals.values()):
-        settle(send_sem.at[6 + i], rows, count * below, values)
+    for i, departure in enumerate(departures):
+        settle(send_sem.at[i], *departure)
 
 
 def finish(fv, mv, f_hbm, m_hbm, sem):
@@ -648,7 +662,7 @@
     kept = pl.pallas_call(
         functools.partial(kernel, (X, Y, Z), sizes),
         out_shape=(vmem((6, N, Z), f32), vmem((3, N, Z), f32)),
-        in_specs=[any_space] * 5,
+        in_specs=[any_space] * 6,
         out_specs=(in_vmem, in_vmem),
         scratch_shapes=[
             vmem((3, N + 2 * Y, Z), f32),
@@ -664,7 +678,7 @@
             vmem((6, N + 2 * Y, Z), f32),
             vmem((2, 8, Y, Z), f32),
             vmem((2, 8, X, Z), f32),
-            vmem((2, 3, X, Z), f32),
+            vmem((3, X, Z), f32),
             vmem((2, W, Z), f32),
             vmem((2, Y, Z), f32),
             vmem((2, 2, 8, Z), f32),
@@ -678,20 +692,20 @@
             vmem((2, Y, Z), f32),
             vmem((2, 2, Y, Z), f32),
             vmem((2, 2, 8, Z), f32),
-            vmem((2, 2, Y, Z), f32),
+            vmem((2, 2, 3, Y, Z), f32),
             vmem((2, 2, 2, W, Z), f32),
             vmem((D, Y, Z), f32),
             vmem((2, D, Y, Z), f32),
             vmem((2, D, X, Z), f32),
             dma((4,)),
             pltpu.SemaphoreType.REGULAR((4,)),
-            pltpu.SemaphoreType.REGULAR((1,)),
+            pltpu.SemaphoreType.REGULAR((1 if layers == 2 else 2,)),
+            dma((6,)),
             dma((9,)),
-            dma((12,)),
         ],
         compiler_params=pltpu.CompilerParams(collective_id=0, has_side_effects=True),
         name="strain_step",
-    )(u.reshape(3, N, Z), e.reshape(6, N, Z), t.reshape(N, Z), r.reshape(N, Z), b.reshape(N, Z))
+    )(u.reshape(3, N, Z), u, e.reshape(6, N, Z), t.reshape(N, Z), r.reshape(N, Z), b.reshape(N, Z))
     f, m = pl.pallas_call(
         finish,
         out_shape=(jax.ShapeDtypeStruct((6, N, Z), f32), jax.ShapeDtypeStruct((3, N, Z), f32)),

time: 10.3 us -> 9.9 us (0.961)
  the two profiles are of different devices: /device:TPU:19 before, /device:TPU:20 now
where the time goes in v5:
time: 9.9 us; the launch traced here: 9.75 us
  Pallas kernels  9.11 us (92%)
  between operations  0.64 us (6%)
    pallas_call x1, Pallas kernels, shards(): pl.pallas_call(functools.partial(kernel, (X, Y, Z), sizes), out_shape=(vm...  8.08 us
    pallas_call x1, Pallas kernels, shards(): pl.pallas_call(finish, out_shape=(jax.ShapeDtypeStruct((6, N, Z), f32), j...  1.03 us

profile of v5, /device:TPU:20, one launch (start us, length us, event | category | flops | bytes accessed | tf_op | source)
XLA Modules:
  0.0 9.8 jit_solution(8775657919544014816)
XLA Ops:
  0.6 8.1 %strain_step.1 = (f32[6,256,128]{2,1,0:T(8,128)S(1)}, f32[3,256,128]{2,1,0:T(8,128)S(1)}) custom-call(f32[3,256,128]{2,1,0:T(8,128)} %bitcast.7, f32[3,16,16,128]{3,2,1,0:T(8,128)} %u_rows.1, f32[6,256,128]{2,1,0:T(8,128)} %bitcast.8, f32[256,128]{1,0:T(8,128)} %bitcast.9, f32[256,128]{1,0:T(8,128)} %bitcast.10, s32[256,128]{1,0:T(8,128)} %bitcast.11), custom_call_target="tpu_custom_call" | custom-call | tf_op jit(solution)/shard_map/strain_step/pallas_call | solution.py:662
  8.7 1.0 %finish.1 = (f32[6,256,128]{2,1,0:T(8,128)}, f32[3,256,128]{2,1,0:T(8,128)}) custom-call(f32[6,256,128]{2,1,0:T(8,128)S(1)} %get-tuple-element.6.fv, f32[3,256,128]{2,1,0:T(8,128)S(1)} %get-tuple-element.7.mv), custom_call_target="tpu_custom_call" | custom-call | tf_op jit(solution)/shard_map/finish/pallas_call | solution.py:709

commit v6 on v5

--- a/solution.py
+++ b/solution.py
@@ -85,7 +85,7 @@
 def kernel(
     dims, sizes,
     u_hbm, u_rows, e_hbm, t_hbm, r_hbm, b_hbm,
-    fv, mv,
+    fv, mv, jv,
     uv, ev, tv, rv, bv, pv, tot, el, av, nt, sp,
     xs, ys, yu, zu, zs, xy, zt, xt, yt,
     rxu, rxs, ryu, rys, rzu, rzs, rxy, rxz, ryz, rt, rtx, rty,
@@ -419,16 +419,15 @@
     loads[6].wait()
     for x in inner:
         elastic(x, tiles)
+    for k in range(2):
+        zs[k] = tiles[k]
+    start(lowers, ("zs",))
     for i, line in enumerate((0, Y - 1)):
         for k in range(8):
             src = el.at[k] if k < 6 else (av, nt)[k - 6]
             ys[i, k] = src[pl.ds(line, X, stride=Y), :]
     start(lowers, ("ys",))
-    for k in range(2):
-        zs[k] = tiles[k]
-    start(lowers, ("zs",))
-
-    everything = ("zu", "yu", "xu", "t", "zs", "ys", "xs", "tx", "ty", "xy", "xz", "yz")
+
     near = [o for o in uppers if sum(o) == 1]
     for o in sorted(near):
         @pl.when(has[o])
@@ -439,11 +438,14 @@
         low, high = split(o)
         if high in near and minus(low) in near:
             announce(o)
-    start(sorted(near), everything)
+    near.sort()
+    start(near, ("zu", "yu", "xu", "t", "zs"))
     others = [o for o in uppers if o not in near]
     far = [o for o in mixed if split(o)[1] not in near or minus(split(o)[0]) not in near]
     close = [o for o in mixed if o not in far]
 
+    diagonal = ("xy", "xz", "yz", "t", "tx", "ty")
+
     def hear(offsets_in, sem):
         number = sum(has[o].astype(jnp.int32) for o in offsets_in)
 
@@ -451,9 +453,10 @@
         def _():
             pl.semaphore_wait(sem, number)
 
-        start(offsets_in, everything)
+        start(offsets_in, diagonal)
 
     hear(close, told.at[0])
+    start(near, ("ys", "xs"))
     hear(others, ready.at[3])
     for o in far:
         announce(o)
@@ -597,11 +600,7 @@
     for c in range(3):
         tile = shift(stress(e, change, trace, Z_SET[c]) * known, c * block)
         gathered = jnp.where((pair >= c * X) & (pair < (c + 1) * X), tile, gathered)
-    joined = jnp.where(even, gathered, shift(gathered, -2))
-    for c in range(3):
-        for x in range(X):
-            own = pl.ds(x * Y, Y)
-            mv[c, own, :] = mv[c, own, :] + edge_term(joined, c * X + x, z_edge)
+    jv[...] = jnp.where(even, gathered, shift(gathered, -2))
 
     @pl.when(jnp.logical_not(first_row))
     def _():
@@ -636,13 +635,23 @@
         settle(send_sem.at[i], *departure)
 
 
-def finish(fv, mv, f_hbm, m_hbm, sem):
-    copies = [
-        pltpu.make_async_copy(mv, m_hbm, sem.at[0]),
-        pltpu.make_async_copy(fv, f_hbm, sem.at[1]),
-    ]
-    for copy in copies:
-        copy.start()
+def finish(dims, fv, mv, jv, f_hbm, m_hbm, ms, sem):
+    X, Y, Z = dims
+    copies = [pltpu.make_async_copy(fv, f_hbm, sem.at[0])]
+    copies[0].start()
+    lane = lax.broadcasted_iota(jnp.int32, (Y, Z), 1)
+    z_edge = jnp.where(lane == 0, -0.5, jnp.where(lane == Z - 1, 0.5, 0.0)).astype(jnp.float32)
+    joined = jv[...]
+    groups = 4
+    span = X // groups
+    for g in range(groups):
+        for x in range(g * span, (g + 1) * span):
+            own = pl.ds(x * Y, Y)
+            for c in range(3):
+                ms[c, own, :] = mv[c, own, :] + edge_term(joined, c * X + x, z_edge)
+        rows = pl.ds(g * span * Y, span * Y)
+        copies.append(pltpu.make_async_copy(ms.at[:, rows, :], m_hbm.at[:, rows, :], sem.at[1 + g]))
+        copies[-1].start()
     for copy in copies:
         copy.wait()
 
@@ -661,9 +670,9 @@
     D = max(layers - 1, 1)
     kept = pl.pallas_call(
         functools.partial(kernel, (X, Y, Z), sizes),
-        out_shape=(vmem((6, N, Z), f32), vmem((3, N, Z), f32)),
+        out_shape=(vmem((6, N, Z), f32), vmem((3, N, Z), f32), vmem((Y, Z), f32)),
         in_specs=[any_space] * 6,
-        out_specs=(in_vmem, in_vmem),
+        out_specs=(in_vmem,) * 3,
         scratch_shapes=[
             vmem((3, N + 2 * Y, Z), f32),
             vmem((6, N, Z), f32),
@@ -707,11 +716,11 @@
         name="strain_step",
     )(u.reshape(3, N, Z), u, e.reshape(6, N, Z), t.reshape(N, Z), r.reshape(N, Z), b.reshape(N, Z))
     f, m = pl.pallas_call(
-        finish,
+        functools.partial(finish, (X, Y, Z)),
         out_shape=(jax.ShapeDtypeStruct((6, N, Z), f32), jax.ShapeDtypeStruct((3, N, Z), f32)),
-        in_specs=[in_vmem] * 2,
+        in_specs=[in_vmem] * 3,
         out_specs=(any_space, any_space),
-        scratch_shapes=[dma((2,))],
+        scratch_shapes=[vmem((3, N, Z), f32), dma((5,))],
         name="finish",
     )(*(pltpu.with_memory_space_constraint(k, vmem) for k in kept))
     return f.reshape(6, X, Y, Z), m.reshape(3, X, Y, Z)

time: 9.9 us -> 9.56 us (0.966)
  the two profiles are of different devices: /device:TPU:20 before, /device:TPU:0 now
where the time goes in v6:
time: 9.56 us; the launch traced here: 9.38 us
  Pallas kernels  8.74 us (91%)
  between operations  0.64 us (7%)
    pallas_call x1, Pallas kernels, shards(): pl.pallas_call(functools.partial(kernel, (X, Y, Z), sizes), out_shape=(vm...  7.7 us
    pallas_call x1, Pallas kernels, shards(): pl.pallas_call(functools.partial(finish, (X, Y, Z)), out_shape=(jax.Shape...  1.04 us

profile of v6, /device:TPU:0, one launch (start us, length us, event | category | flops | bytes accessed | tf_op | source)
XLA Modules:
  0.0 9.4 jit_solution(14039050535449567130)
XLA Ops:
  0.6 7.7 %strain_step.1 = (f32[6,256,128]{2,1,0:T(8,128)S(1)}, f32[3,256,128]{2,1,0:T(8,128)S(1)}, f32[16,128]{1,0:T(8,128)S(1)}) custom-call(f32[3,256,128]{2,1,0:T(8,128)} %bitcast.7, f32[3,16,16,128]{3,2,1,0:T(8,128)} %u_rows.1, f32[6,256,128]{2,1,0:T(8,128)} %bitcast.8, f32[256,128]{1,0:T(8,128)} %bitcast.9, f32[256,128]{1,0:T(8,128)} %bitcast.10, ...), custom_call_target="tpu_custom_call" | custom-call | tf_op jit(solution)/shard_map/strain_step/pallas_call | solution.py:671
  8.3 1.0 %finish.1 = (f32[6,256,128]{2,1,0:T(8,128)}, f32[3,256,128]{2,1,0:T(8,128)}) custom-call(f32[6,256,128]{2,1,0:T(8,128)S(1)} %get-tuple-element.7.fv, f32[3,256,128]{2,1,0:T(8,128)S(1)} %get-tuple-element.8.mv, f32[16,128]{1,0:T(8,128)S(1)} %get-tuple-element.9.jv), custom_call_target="tpu_custom_call" | custom-call | tf_op jit(solution)/shard_map/finish/pallas_call | solution.py:718

commit v7 on v6

--- a/solution.py
+++ b/solution.py
@@ -442,7 +442,7 @@
     start(near, ("zu", "yu", "xu", "t", "zs"))
     others = [o for o in uppers if o not in near]
     far = [o for o in mixed if split(o)[1] not in near or minus(split(o)[0]) not in near]
-    close = [o for o in mixed if o not in far]
+    close = sorted((o for o in mixed if o not in far), key=lambda o: (abs(o[0]), abs(o[2])))
 
     diagonal = ("xy", "xz", "yz", "t", "tx", "ty")
 
@@ -528,38 +528,49 @@
     def ends_of(first, last, rows, count):
         return jnp.where(rows == 0, -first, jnp.where(rows == count - 1, last, 0.0))
 
-    def along_gy():
-        arrive("ys")
-        for side, line in enumerate((0, Y - 1)):
-            @pl.when(has[faces[1][side]])
-            def _(side=side, line=line):
-                e = [rys[side, k] for k in range(6)]
-                add(e, 1, 1.0 - 2.0 * side, [uv[c, pl.ds(Y + line, X, stride=Y), :] for c in range(3)])
-                add(e, 0, 1.0, [
-                    ends_of(rxy[0, side, pl.ds(c, 1), :], rxy[1, side, pl.ds(c, 1), :], row_x, X) for c in range(3)
-                ])
-                joined = merge(ryz[side, 0, 1, pl.ds(0, X), :], ryz[side, 1, 1, pl.ds(0, X), :])
-                add(e, 2, 2.0, [edge_term(joined, 3 * (1 - side) + c, z_edge_x) for c in range(3)])
-                load = row_plane
-                for d in depths:
-                    load = load + rty[side, d - 1]
-                trace, change = flow(e, rys[side, 6] * jnp.exp(load * rys[side, 7]))
-                own = pl.ds(line, X, stride=Y)
-                for c in range(3):
-                    mv[c, own, :] = mv[c, own, :] + (side - 0.5) * stress(e, change, trace, Y_SET[c])
-
-    first_row = me[1] == 0
-
-    @pl.when(first_row)
-    def _():
-        arrive("xy", "yz")
-        along_gy()
-
-    @pl.when(jnp.logical_not(first_row))
-    def _():
-        arrive("yz")
-
-    arrive("zs", "xz")
+    arrive("xy", "yz", "xz", "ys", "zs", "xs")
+
+    def beyond(axis, side, part):
+        got, load, e = part
+        trace, change = flow(e, got[6] * jnp.exp(load * got[7]))
+        there = has[faces[axis][side]]
+        return [
+            (side - 0.5) * jnp.where(there, stress(e, change, trace, k), 0.0) for k in (X_SET, Y_SET)[axis]
+        ]
+
+    along_y = []
+    for side, line in enumerate((0, Y - 1)):
+        e = [rys[side, k] for k in range(6)]
+        add(e, 1, 1.0 - 2.0 * side, [uv[c, pl.ds(Y + line, X, stride=Y), :] for c in range(3)])
+        add(e, 0, 1.0, [
+            ends_of(rxy[0, side, pl.ds(c, 1), :], rxy[1, side, pl.ds(c, 1), :], row_x, X) for c in range(3)
+        ])
+        joined = merge(ryz[side, 0, 1, pl.ds(0, X), :], ryz[side, 1, 1, pl.ds(0, X), :])
+        add(e, 2, 2.0, [edge_term(joined, 3 * (1 - side) + c, z_edge_x) for c in range(3)])
+        load = row_plane
+        for d in depths:
+            load = load + rty[side, d - 1]
+        along_y.append(beyond(1, side, (rys[side], load, e)))
+
+    along_x = []
+    for side, at in enumerate((0, X - 1)):
+        e = [rxs[side, k] for k in range(6)]
+        add(e, 0, 1.0 - 2.0 * side, [uv[c, pl.ds(Y + at * Y, Y), :] for c in range(3)])
+        add(e, 1, 1.0, [
+            ends_of(rxy[side, 0, pl.ds(c, 1), :], rxy[side, 1, pl.ds(c, 1), :], row, Y) for c in range(3)
+        ])
+        add(e, 2, 1.0, [
+            jnp.where(
+                lane == 0, -pltpu.roll(rxz[side, 0, c], 1, 1),
+                jnp.where(lane == Z - 1, pltpu.roll(rxz[side, 1, c], Z - 1, 1), 0.0),
+            )
+            for c in range(3)
+        ])
+        load = plane
+        for d in depths:
+            load = load + rtx[side, d - 1]
+        along_x.append(beyond(0, side, (rxs[side], load, e)))
+
     block = 2 * X
 
     def shift(tile, by):
@@ -602,35 +613,14 @@
         gathered = jnp.where((pair >= c * X) & (pair < (c + 1) * X), tile, gathered)
     jv[...] = jnp.where(even, gathered, shift(gathered, -2))
 
-    @pl.when(jnp.logical_not(first_row))
-    def _():
-        arrive("xy")
-
-    arrive("xs")
-    for side, at in enumerate((0, X - 1)):
-        @pl.when(has[faces[0][side]])
-        def _(side=side, at=at):
-            e = [rxs[side, k] for k in range(6)]
-            add(e, 0, 1.0 - 2.0 * side, [uv[c, pl.ds(Y + at * Y, Y), :] for c in range(3)])
-            add(e, 1, 1.0, [
-                ends_of(rxy[side, 0, pl.ds(c, 1), :], rxy[side, 1, pl.ds(c, 1), :], row, Y) for c in range(3)
-            ])
-            add(e, 2, 1.0, [
-                jnp.where(
-                    lane == 0, -pltpu.roll(rxz[side, 0, c], 1, 1),
-                    jnp.where(lane == Z - 1, pltpu.roll(rxz[side, 1, c], Z - 1, 1), 0.0),
-                )
-                for c in range(3)
-            ])
-            load = plane
-            for d in depths:
-                load = load + rtx[side, d - 1]
-            trace, change = flow(e, rxs[side, 6] * jnp.exp(load * rxs[side, 7]))
+    for c in range(3):
+        for side, at in enumerate((0, X - 1)):
             own = pl.ds(at * Y, Y)
-            for c in range(3):
-                mv[c, own, :] = mv[c, own, :] + (side - 0.5) * stress(e, change, trace, X_SET[c])
-
-    pl.when(jnp.logical_not(first_row))(along_gy)
+            mv[c, own, :] = mv[c, own, :] + along_x[side][c]
+        for side, line in enumerate((0, Y - 1)):
+            own = pl.ds(line, X, stride=Y)
+            mv[c, own, :] = mv[c, own, :] + along_y[side][c]
+
     for i, departure in enumerate(departures):
         settle(send_sem.at[i], *departure)
 

time: 9.56 us -> 9.42 us (0.985)
  Pallas kernels: 8.74 us -> 8.64 us
    pallas_call x1, Pallas kernels: 7.7 us -> 7.6 us  [shards(): pl.pallas_call(functools.partial(kernel, (X, Y, Z), sizes), out_shape=(vm...]
where the time goes in v7:
time: 9.42 us; the launch traced here: 9.28 us
  Pallas kernels  8.64 us (92%)
  between operations  0.64 us (7%)
    pallas_call x1, Pallas kernels, shards(): pl.pallas_call(functools.partial(kernel, (X, Y, Z), sizes), out_shape=(vm...  7.6 us
    pallas_call x1, Pallas kernels, shards(): pl.pallas_call(functools.partial(finish, (X, Y, Z)), out_shape=(jax.Shape...  1.04 us

profile of v7, /device:TPU:0, one launch (start us, length us, event | category | flops | bytes accessed | tf_op | source)
XLA Modules:
  0.0 9.3 jit_solution(3247850985111138981)
XLA Ops:
  0.6 7.6 %strain_step.1 = (f32[6,256,128]{2,1,0:T(8,128)S(1)}, f32[3,256,128]{2,1,0:T(8,128)S(1)}, f32[16,128]{1,0:T(8,128)S(1)}) custom-call(f32[3,256,128]{2,1,0:T(8,128)} %bitcast.7, f32[3,16,16,128]{3,2,1,0:T(8,128)} %u_rows.1, f32[6,256,128]{2,1,0:T(8,128)} %bitcast.8, f32[256,128]{1,0:T(8,128)} %bitcast.9, f32[256,128]{1,0:T(8,128)} %bitcast.10, ...), custom_call_target="tpu_custom_call" | custom-call | tf_op jit(solution)/shard_map/strain_step/pallas_call | solution.py:661
  8.2 1.0 %finish.1 = (f32[6,256,128]{2,1,0:T(8,128)}, f32[3,256,128]{2,1,0:T(8,128)}) custom-call(f32[6,256,128]{2,1,0:T(8,128)S(1)} %get-tuple-element.7.fv, f32[3,256,128]{2,1,0:T(8,128)S(1)} %get-tuple-element.8.mv, f32[16,128]{1,0:T(8,128)S(1)} %get-tuple-element.9.jv), custom_call_target="tpu_custom_call" | custom-call | tf_op jit(solution)/shard_map/finish/pallas_call | solution.py:708

commit v8 on v7

--- a/solution.py
+++ b/solution.py
@@ -86,7 +86,7 @@
     dims, sizes,
     u_hbm, u_rows, e_hbm, t_hbm, r_hbm, b_hbm,
     fv, mv, jv,
-    uv, ev, tv, rv, bv, pv, tot, el, av, nt, sp,
+    uv, tri, ev, tv, rv, bv, pv, tot, el, av, nt, sp,
     xs, ys, yu, zu, zs, xy, zt, xt, yt,
     rxu, rxs, ryu, rys, rzu, rzs, rxy, rxz, ryz, rt, rtx, rty,
     in_sem, ready, told, send_sem, recv_sem,
@@ -136,7 +136,8 @@
         copy.start()
 
     def take(sem, rows):
-        planes = next(k for k in range(1, 7) if rows % (8 * k) == 0 and rows // k <= N + 2 * Y)
+        whole = [k for k in range(1, 7) if rows % (8 * k) == 0 and rows // k <= N + 2 * Y]
+        planes = whole[0] if whole else rows // 3
         spot = sp.at[pl.ds(0, planes), pl.ds(0, rows // planes)]
         pltpu.make_async_copy(spot, spot, sem).wait()
 
@@ -177,6 +178,15 @@
         for j, s in enumerate((-1, 1)):
             blank((s, 0, -d), rtx.at[j, d - 1])
             blank((0, s, -d), rty.at[j, d - 1])
+
+    above_row = lax.broadcasted_iota(jnp.int32, (Z, 2 * Z), 0)
+    column = lax.broadcasted_iota(jnp.int32, (Z, 2 * Z), 1)
+    triangle = jnp.where(
+        (above_row < column) | (column >= Z),
+        1.0,
+        jnp.where(above_row == column, 0.5, 0.0),
+    ).astype(jnp.bfloat16)
+    tri[...] = triangle
 
     lane = lax.broadcasted_iota(jnp.int32, (Y, Z), 1)
     row = lax.broadcasted_iota(jnp.int32, (Y, Z), 0)
@@ -212,7 +222,7 @@
         "ys": (X, beside[1] * (8 + above), products(some, [8 + d for d in any_depth])),
         "zu": (Y, beside[2] + above, sorted({n + d for n in some for d in any_depth})),
         "zs": (2 * Y, beside[2], some),
-        "xy": (8, beside[0] * beside[1], four),
+        "xy": (3, beside[0] * beside[1], four),
         "xz": (3 * Y, beside[0] * beside[2], four),
         "yz": (2 * W, beside[1] * beside[2], four),
     }
@@ -248,7 +258,8 @@
         message("zs", (0, 0, s), zs, rzs.at[k])
         for j, s2 in enumerate((-1, 1)):
             m = 1 - j
-            message("xy", (s, s2, 0), xy.at[i, j], rxy.at[k, m])
+            lines = xy.at[i, j, pl.ds(0, 3), :] if s + s2 >= 0 else u_rows.at[:, 0, 0, :]
+            message("xy", (s, s2, 0), lines, rxy.at[k, m, pl.ds(0, 3), :])
             strike = u_hbm.at[:, pl.ds(0, Y), :] if s + s2 < 0 else uv.at[:, pl.ds(at, Y), :]
             message("xz", (s, 0, s2), strike, rxz.at[k, m])
             message("yz", (0, s, s2), zu, ryz.at[k, m])
@@ -297,10 +308,89 @@
             pl.semaphore_signal(told.at[kind], inc=1, device_id=partner(minus(low)), device_id_type=MESH)
 
     lowers = sorted(lowers, key=lambda o: (sum(map(abs, o)), o[2], o[1]))
-    for kind in ("xz", "yu", "xu"):
+    for kind in ("xz", "yu", "xy", "xu"):
         start(lowers, (kind,))
 
     loads[0].wait()
+    loads[1].wait()
+    total_depth = Z * layers
+    depth = (me[2] * Z + lane).astype(jnp.float32)
+    scale = (1.0 + 2.0 * depth / total_depth) / total_depth
+
+    def prefix(planes):
+        thirds = [[], [], []]
+        for x in planes:
+            rest = rv[pl.ds(x * Y, Y), :] * scale
+            for k in range(3):
+                piece = rest.astype(jnp.bfloat16)
+                thirds[k].append(piece)
+                rest = rest - piece.astype(jnp.float32)
+        weight = jnp.concatenate([jnp.concatenate(k, axis=0) for k in thirds], axis=1)
+        triangle = jnp.concatenate([tri[...]] * 3, axis=0)
+        sums = jnp.dot(weight, triangle, preferred_element_type=jnp.float32)
+        for i, x in enumerate(planes):
+            pv[pl.ds(x * Y, Y), :] = sums[i * Y:(i + 1) * Y, :Z] + 1.0
+            tot[pl.ds(x * Y, Y), :] = sums[i * Y:(i + 1) * Y, Z:]
+
+    tiles = [plane, plane]
+
+    def strain(x):
+        base = Y + x * Y
+        own = pl.ds(x * Y, Y)
+        grad = []
+        for c in range(3):
+            here = uv[c, pl.ds(base, Y), :]
+            grad.append((
+                (uv[c, pl.ds(base + Y, Y), :] - uv[c, pl.ds(base - Y, Y), :]) * 0.5,
+                uv[c, pl.ds(base + 1, Y), :] * not_last - uv[c, pl.ds(base - 1, Y), :] * not_first,
+                pltpu.roll(here, Z - 1, 1) * z_last - pltpu.roll(here, 1, 1) * z_first,
+            ))
+        el[0, own, :] = grad[0][0]
+        el[1, own, :] = grad[1][1]
+        el[2, own, :] = grad[2][2]
+        el[3, own, :] = 0.5 * (grad[0][1] + grad[1][0])
+        el[4, own, :] = 0.5 * (grad[0][2] + grad[2][0])
+        el[5, own, :] = 0.5 * (grad[1][2] + grad[2][1])
+
+    def pack(k, x, part, tiles):
+        q = (k % 4) * X + x
+        tile = pltpu.roll(part, (2 * q + 1) % Z, 1)
+        tiles[k // 4] = jnp.where(pair == q, tile, tiles[k // 4])
+
+    def factors(x, tiles):
+        own = pl.ds(x * Y, Y)
+        minus_two = -2.0 / tv[own, :]
+        factor = (2.0 + 14.0 * bv[own, :].astype(jnp.float32)) * jnp.exp(pv[own, :] * minus_two)
+        av[own, :] = factor
+        nt[own, :] = minus_two
+        for i, at in enumerate((0, X - 1)):
+            if x == at:
+                xs[i, 6] = factor
+                xs[i, 7] = minus_two
+        pack(6, x, factor, tiles)
+        pack(7, x, minus_two, tiles)
+
+    def elastic(x, tiles):
+        own = pl.ds(x * Y, Y)
+        for k in range(6):
+            part = el[k, own, :] - ev[k, own, :]
+            el[k, own, :] = part
+            for i, at in enumerate((0, X - 1)):
+                if x == at:
+                    xs[i, k] = part
+            pack(k, x, part, tiles)
+
+    ends = sorted({0, X - 1})
+    inner = [x for x in range(X) if x not in ends]
+    prefix(ends)
+    for x in ends:
+        strain(x)
+    take(in_sem.at[2], 12 * Y + 2 * N)
+    for x in ends:
+        elastic(x, tiles)
+        factors(x, tiles)
+    start(lowers, ("xs",))
+
     tile0 = plane
     for x in range(X):
         for c in range(3):
@@ -322,31 +412,9 @@
                 xy[j, i, pl.ds(c, 1), :] = uv[c, pl.ds(Y + at * Y + line, 1), :]
     zu[1, pl.ds(0, X), :] = tile
 
-    start(lowers, ("xy", "yz"))
-
-    loads[1].wait()
-    total_depth = Z * layers
-    depth = (me[2] * Z + lane).astype(jnp.float32)
-    scale = (1.0 + 2.0 * depth / total_depth) / total_depth
-    thirds = [[], [], []]
-    for x in range(X):
-        rest = rv[pl.ds(x * Y, Y), :] * scale
-        for k in range(3):
-            piece = rest.astype(jnp.bfloat16)
-            thirds[k].append(piece)
-            rest = rest - piece.astype(jnp.float32)
-    weight = jnp.concatenate([jnp.concatenate(k, axis=0) for k in thirds], axis=1)
-    above_row = lax.broadcasted_iota(jnp.int32, (Z, 2 * Z), 0)
-    column = lax.broadcasted_iota(jnp.int32, (Z, 2 * Z), 1)
-    triangle = jnp.where(
-        (above_row < column) | (column >= Z),
-        1.0,
-        jnp.where(above_row == column, 0.5, 0.0),
-    ).astype(jnp.bfloat16)
-    triangle = jnp.concatenate([triangle] * 3, axis=0)
-    sums = jnp.dot(weight, triangle, preferred_element_type=jnp.float32)
-    pv[...] = sums[:, :Z] + 1.0
-    tot[...] = sums[:, Z:]
+    start(lowers, ("yz",))
+
+    prefix(inner)
     tile = plane
     for x in range(X):
         tile = jnp.where(pair == x, tot[pl.ds(x * Y, Y), :], tile)
@@ -355,73 +423,15 @@
         xt[i] = tot[pl.ds(at * Y, Y), :]
         yt[i] = tot[pl.ds(line, X, stride=Y), :]
 
-    tiles = [plane, plane]
-
-    def strain(x):
-        base = Y + x * Y
-        own = pl.ds(x * Y, Y)
-        grad = []
-        for c in range(3):
-            here = uv[c, pl.ds(base, Y), :]
-            grad.append((
-                (uv[c, pl.ds(base + Y, Y), :] - uv[c, pl.ds(base - Y, Y), :]) * 0.5,
-                uv[c, pl.ds(base + 1, Y), :] * not_last - uv[c, pl.ds(base - 1, Y), :] * not_first,
-                pltpu.roll(here, Z - 1, 1) * z_last - pltpu.roll(here, 1, 1) * z_first,
-            ))
-        el[0, own, :] = grad[0][0]
-        el[1, own, :] = grad[1][1]
-        el[2, own, :] = grad[2][2]
-        el[3, own, :] = 0.5 * (grad[0][1] + grad[1][0])
-        el[4, own, :] = 0.5 * (grad[0][2] + grad[2][0])
-        el[5, own, :] = 0.5 * (grad[1][2] + grad[2][1])
-
-    def pack(k, x, part, tiles):
-        q = (k % 4) * X + x
-        tile = pltpu.roll(part, (2 * q + 1) % Z, 1)
-        tiles[k // 4] = jnp.where(pair == q, tile, tiles[k // 4])
-
-    def factors(x, tiles):
-        own = pl.ds(x * Y, Y)
-        minus_two = -2.0 / tv[own, :]
-        factor = (2.0 + 14.0 * bv[own, :].astype(jnp.float32)) * jnp.exp(pv[own, :] * minus_two)
-        av[own, :] = factor
-        nt[own, :] = minus_two
-        for i, at in enumerate((0, X - 1)):
-            if x == at:
-                xs[i, 6] = factor
-                xs[i, 7] = minus_two
-        pack(6, x, factor, tiles)
-        pack(7, x, minus_two, tiles)
-
-    def elastic(x, tiles):
-        own = pl.ds(x * Y, Y)
-        for k in range(6):
-            part = el[k, own, :] - ev[k, own, :]
-            el[k, own, :] = part
-            for i, at in enumerate((0, X - 1)):
-                if x == at:
-                    xs[i, k] = part
-            pack(k, x, part, tiles)
-
-    ends = sorted({0, X - 1})
-    for x in ends:
-        strain(x)
-    take(in_sem.at[2], 12 * Y + 2 * N)
-    for x in ends:
-        elastic(x, tiles)
-        factors(x, tiles)
-    start(lowers, ("xs", "t", "tx", "ty"))
-
-    inner = [x for x in range(X) if x not in ends]
     for x in inner:
         strain(x)
-        factors(x, tiles)
     loads[6].wait()
     for x in inner:
         elastic(x, tiles)
+        factors(x, tiles)
     for k in range(2):
         zs[k] = tiles[k]
-    start(lowers, ("zs",))
+    start(lowers, ("zs", "t", "tx", "ty"))
     for i, line in enumerate((0, Y - 1)):
         for k in range(8):
             src = el.at[k] if k < 6 else (av, nt)[k - 6]
@@ -665,6 +675,7 @@
         out_specs=(in_vmem,) * 3,
         scratch_shapes=[
             vmem((3, N + 2 * Y, Z), f32),
+            vmem((Z, 2 * Z), jnp.bfloat16),
             vmem((6, N, Z), f32),
             vmem((N, Z), f32),
             vmem((N, Z), f32),

time: 9.42 us -> 9.41 us (level)
  no operation moved by 1% of the time
where the time goes in v8:
time: 9.41 us; the launch traced here: 9.26 us
  Pallas kernels  8.63 us (92%)
  between operations  0.64 us (7%)
    pallas_call x1, Pallas kernels, shards(): pl.pallas_call(functools.partial(kernel, (X, Y, Z), sizes), out_shape=(vm...  7.58 us
    pallas_call x1, Pallas kernels, shards(): pl.pallas_call(functools.partial(finish, (X, Y, Z)), out_shape=(jax.Shape...  1.04 us

profile of v8, /device:TPU:0, one launch (start us, length us, event | category | flops | bytes accessed | tf_op | source)
XLA Modules:
  0.0 9.3 jit_solution(14767133635541418602)
XLA Ops:
  0.6 7.6 %strain_step.1 = (f32[6,256,128]{2,1,0:T(8,128)S(1)}, f32[3,256,128]{2,1,0:T(8,128)S(1)}, f32[16,128]{1,0:T(8,128)S(1)}) custom-call(f32[3,256,128]{2,1,0:T(8,128)} %bitcast.7, f32[3,16,16,128]{3,2,1,0:T(8,128)} %u_rows.1, f32[6,256,128]{2,1,0:T(8,128)} %bitcast.8, f32[256,128]{1,0:T(8,128)} %bitcast.9, f32[256,128]{1,0:T(8,128)} %bitcast.10, ...), custom_call_target="tpu_custom_call" | custom-call | tf_op jit(solution)/shard_map/strain_step/pallas_call | solution.py:671
  8.2 1.0 %finish.1 = (f32[6,256,128]{2,1,0:T(8,128)}, f32[3,256,128]{2,1,0:T(8,128)}) custom-call(f32[6,256,128]{2,1,0:T(8,128)S(1)} %get-tuple-element.7.fv, f32[3,256,128]{2,1,0:T(8,128)S(1)} %get-tuple-element.8.mv, f32[16,128]{1,0:T(8,128)S(1)} %get-tuple-element.9.jv), custom_call_target="tpu_custom_call" | custom-call | tf_op jit(solution)/shard_map/finish/pallas_call | solution.py:719

commit v9 on v8

--- a/solution.py
+++ b/solution.py
@@ -101,7 +101,7 @@
     W = max(X, Y)
 
     def ready_index(o):
-        return o.index(1) if sum(o) == 1 else 3
+        return 0 if sum(o) == 1 else 1
 
     def exists(o):
         ok = None
@@ -119,7 +119,7 @@
     faces = {a: [tuple(s if i == a else 0 for i in range(3)) for s in (-1, 1)] for a in range(3)}
 
     loads = [
-        pltpu.make_async_copy(src, dst, in_sem.at[min(i, 2) if i < 6 else 3])
+        pltpu.make_async_copy(src, dst, in_sem.at[0 if i < 2 else 1 if i < 6 else 2])
         for i, (src, dst) in enumerate(
             (
                 (u_hbm, uv.at[:, pl.ds(Y, N), :]),
@@ -237,12 +237,13 @@
     send_index = {
         "xu": 0, "xs": 0, "tx": 0, "yu": 1, "ys": 1, "ty": 1, "zu": 2, "zs": 2, "t": 2, "xy": 3, "xz": 4, "yz": 5,
     }
+    sent = [send_sem.at[0], send_sem.at[1], in_sem.at[0], send_sem.at[2], send_sem.at[3], send_sem.at[4]]
     sends = {o: [] for o in offs}
 
     def message(kind, o, src, dst):
         sends[o].append((kind, pltpu.make_async_remote_copy(
             src_ref=src, dst_ref=dst,
-            send_sem=send_sem.at[send_index[kind]], recv_sem=recv_sem.at[recv_index[kind]],
+            send_sem=sent[send_index[kind]], recv_sem=recv_sem.at[recv_index[kind]],
             device_id=partner(o), device_id_type=MESH,
         )))
 
@@ -311,8 +312,7 @@
     for kind in ("xz", "yu", "xy", "xu"):
         start(lowers, (kind,))
 
-    loads[0].wait()
-    loads[1].wait()
+    take(in_sem.at[0], 4 * N)
     total_depth = Z * layers
     depth = (me[2] * Z + lane).astype(jnp.float32)
     scale = (1.0 + 2.0 * depth / total_depth) / total_depth
@@ -331,8 +331,6 @@
         for i, x in enumerate(planes):
             pv[pl.ds(x * Y, Y), :] = sums[i * Y:(i + 1) * Y, :Z] + 1.0
             tot[pl.ds(x * Y, Y), :] = sums[i * Y:(i + 1) * Y, Z:]
-
-    tiles = [plane, plane]
 
     def strain(x):
         base = Y + x * Y
@@ -367,8 +365,9 @@
             if x == at:
                 xs[i, 6] = factor
                 xs[i, 7] = minus_two
-        pack(6, x, factor, tiles)
-        pack(7, x, minus_two, tiles)
+        if tiles:
+            pack(6, x, factor, tiles)
+            pack(7, x, minus_two, tiles)
 
     def elastic(x, tiles):
         own = pl.ds(x * Y, Y)
@@ -378,71 +377,111 @@
             for i, at in enumerate((0, X - 1)):
                 if x == at:
                     xs[i, k] = part
-            pack(k, x, part, tiles)
+            if tiles:
+                pack(k, x, part, tiles)
 
     ends = sorted({0, X - 1})
     inner = [x for x in range(X) if x not in ends]
-    prefix(ends)
-    for x in ends:
-        strain(x)
-    take(in_sem.at[2], 12 * Y + 2 * N)
-    for x in ends:
-        elastic(x, tiles)
-        factors(x, tiles)
-    start(lowers, ("xs",))
-
-    tile0 = plane
-    for x in range(X):
-        for c in range(3):
-            q = c * X + x
-            tile = pltpu.roll(uv[c, pl.ds(Y + x * Y, Y), :], (2 * q + 1) % Z, 1)
-            tile0 = jnp.where(pair == q, tile, tile0)
-    zu[0, pl.ds(0, Y), :] = tile0
-    start(lowers, ("zu",))
-    tile = row_plane
-    pair_x = lax.broadcasted_iota(jnp.int32, (X, Z), 1) >> 1
-    for i, line in enumerate((0, Y - 1)):
-        for c in range(3):
-            p = 3 * i + c
-            lines = uv[c, pl.ds(Y + line, X, stride=Y), :]
-            if i:
-                yu[c] = lines
-            tile = jnp.where(pair_x == p, pltpu.roll(lines, (2 * p + 1) % Z, 1), tile)
-            for j, at in enumerate((0, X - 1)):
-                xy[j, i, pl.ds(c, 1), :] = uv[c, pl.ds(Y + at * Y + line, 1), :]
-    zu[1, pl.ds(0, X), :] = tile
-
-    start(lowers, ("yz",))
-
-    prefix(inner)
-    tile = plane
-    for x in range(X):
-        tile = jnp.where(pair == x, tot[pl.ds(x * Y, Y), :], tile)
-    zt[...] = tile
-    for i, (at, line) in enumerate(((0, 0), (X - 1, Y - 1))):
-        xt[i] = tot[pl.ds(at * Y, Y), :]
-        yt[i] = tot[pl.ds(line, X, stride=Y), :]
-
-    for x in inner:
-        strain(x)
-    loads[6].wait()
-    for x in inner:
-        elastic(x, tiles)
-        factors(x, tiles)
-    for k in range(2):
-        zs[k] = tiles[k]
-    start(lowers, ("zs", "t", "tx", "ty"))
-    for i, line in enumerate((0, Y - 1)):
-        for k in range(8):
-            src = el.at[k] if k < 6 else (av, nt)[k - 6]
-            ys[i, k] = src[pl.ds(line, X, stride=Y), :]
-    start(lowers, ("ys",))
+
+    def pack_displacement():
+        tile0 = plane
+        for x in range(X):
+            for c in range(3):
+                q = c * X + x
+                tile = pltpu.roll(uv[c, pl.ds(Y + x * Y, Y), :], (2 * q + 1) % Z, 1)
+                tile0 = jnp.where(pair == q, tile, tile0)
+        zu[0, pl.ds(0, Y), :] = tile0
+
+    def lines_along_depth():
+        tile = row_plane
+        pair_x = lax.broadcasted_iota(jnp.int32, (X, Z), 1) >> 1
+        for i, line in enumerate((0, Y - 1)):
+            for c in range(3):
+                p = 3 * i + c
+                lines = uv[c, pl.ds(Y + line, X, stride=Y), :]
+                if i:
+                    yu[c] = lines
+                tile = jnp.where(pair_x == p, pltpu.roll(lines, (2 * p + 1) % Z, 1), tile)
+                for j, at in enumerate((0, X - 1)):
+                    xy[j, i, pl.ds(c, 1), :] = uv[c, pl.ds(Y + at * Y + line, 1), :]
+        zu[1, pl.ds(0, X), :] = tile
+
+    def total_tiles():
+        tile = plane
+        for x in range(X):
+            tile = jnp.where(pair == x, tot[pl.ds(x * Y, Y), :], tile)
+        zt[...] = tile
+        for i, (at, line) in enumerate(((0, 0), (X - 1, Y - 1))):
+            xt[i] = tot[pl.ds(at * Y, Y), :]
+            yt[i] = tot[pl.ds(line, X, stride=Y), :]
+
+    def along_dip():
+        for i, line in enumerate((0, Y - 1)):
+            for k in range(8):
+                src = el.at[k] if k < 6 else (av, nt)[k - 6]
+                ys[i, k] = src[pl.ds(line, X, stride=Y), :]
+        start(lowers, ("ys",))
+
+    @pl.when(above == 0)
+    def _():
+        prefix(ends)
+        for x in ends:
+            strain(x)
+        take(in_sem.at[1], 12 * Y + 2 * N)
+        for x in ends:
+            elastic(x, None)
+            factors(x, None)
+        start(lowers, ("xs",))
+        prefix(inner)
+        for x in inner:
+            strain(x)
+        loads[6].wait()
+        for x in inner:
+            elastic(x, None)
+            factors(x, None)
+        along_dip()
+        pack_displacement()
+        lines_along_depth()
+        total_tiles()
+        tiles = [plane, plane]
+        for x in range(X):
+            for k in range(8):
+                src = el.at[k] if k < 6 else (av, nt)[k - 6]
+                pack(k, x, src[pl.ds(x * Y, Y), :], tiles)
+        for k in range(2):
+            zs[k] = tiles[k]
+
+    @pl.when(above > 0)
+    def _():
+        pack_displacement()
+        start(lowers, ("zu",))
+        lines_along_depth()
+        start(lowers, ("yz",))
+        prefix(range(X))
+        total_tiles()
+        for x in range(X):
+            strain(x)
+        take(in_sem.at[1], 12 * Y + 2 * N)
+        tiles = [plane, plane]
+        for x in ends:
+            elastic(x, tiles)
+            factors(x, tiles)
+        start(lowers, ("xs",))
+        loads[6].wait()
+        for x in inner:
+            elastic(x, tiles)
+            factors(x, tiles)
+        for k in range(2):
+            zs[k] = tiles[k]
+        start(lowers, ("zs", "t", "tx", "ty"))
+        along_dip()
 
     near = [o for o in uppers if sum(o) == 1]
-    for o in sorted(near):
-        @pl.when(has[o])
-        def _(o=o):
-            pl.semaphore_wait(ready.at[ready_index(o)], 1)
+    number = sum(has[o].astype(jnp.int32) for o in near)
+
+    @pl.when(number > 0)
+    def _():
+        pl.semaphore_wait(ready.at[0], number)
 
     for o in mixed:
         low, high = split(o)
@@ -467,7 +506,7 @@
 
     hear(close, told.at[0])
     start(near, ("ys", "xs"))
-    hear(others, ready.at[3])
+    hear(others, ready.at[1])
     for o in far:
         announce(o)
     if far:
@@ -632,7 +671,7 @@
             mv[c, own, :] = mv[c, own, :] + along_y[side][c]
 
     for i, departure in enumerate(departures):
-        settle(send_sem.at[i], *departure)
+        settle(sent[i], *departure)
 
 
 def finish(dims, fv, mv, jv, f_hbm, m_hbm, ms, sem):
@@ -707,10 +746,10 @@
             vmem((D, Y, Z), f32),
             vmem((2, D, Y, Z), f32),
             vmem((2, D, X, Z), f32),
-            dma((4,)),
-            pltpu.SemaphoreType.REGULAR((4,)),
+            dma((3,)),
+            pltpu.SemaphoreType.REGULAR((2,)),
             pltpu.SemaphoreType.REGULAR((1 if layers == 2 else 2,)),
-            dma((6,)),
+            dma((5,)),
             dma((9,)),
         ],
         compiler_params=pltpu.CompilerParams(collective_id=0, has_side_effects=True),

time: 9.41 us -> 9.33 us (level)
  no operation moved by 1% of the time
where the time goes in v9:
time: 9.33 us; the launch traced here: 9.18 us
  Pallas kernels  8.54 us (92%)
  between operations  0.64 us (7%)
    pallas_call x1, Pallas kernels, shards(): pl.pallas_call(functools.partial(kernel, (X, Y, Z), sizes), out_shape=(vm...  7.5 us
    pallas_call x1, Pallas kernels, shards(): pl.pallas_call(functools.partial(finish, (X, Y, Z)), out_shape=(jax.Shape...  1.04 us

profile of v9, /device:TPU:0, one launch (start us, length us, event | category | flops | bytes accessed | tf_op | source)
XLA Modules:
  0.0 9.2 jit_solution(12281344229175684130)
XLA Ops:
  0.6 7.5 %strain_step.1 = (f32[6,256,128]{2,1,0:T(8,128)S(1)}, f32[3,256,128]{2,1,0:T(8,128)S(1)}, f32[16,128]{1,0:T(8,128)S(1)}) custom-call(f32[3,256,128]{2,1,0:T(8,128)} %bitcast.7, f32[3,16,16,128]{3,2,1,0:T(8,128)} %u_rows.1, f32[6,256,128]{2,1,0:T(8,128)} %bitcast.8, f32[256,128]{1,0:T(8,128)} %bitcast.9, f32[256,128]{1,0:T(8,128)} %bitcast.10, ...), custom_call_target="tpu_custom_call" | custom-call | tf_op jit(solution)/shard_map/strain_step/pallas_call | solution.py:710
  8.1 1.0 %finish.1 = (f32[6,256,128]{2,1,0:T(8,128)}, f32[3,256,128]{2,1,0:T(8,128)}) custom-call(f32[6,256,128]{2,1,0:T(8,128)S(1)} %get-tuple-element.7.fv, f32[3,256,128]{2,1,0:T(8,128)S(1)} %get-tuple-element.8.mv, f32[16,128]{1,0:T(8,128)S(1)} %get-tuple-element.9.jv), custom_call_target="tpu_custom_call" | custom-call | tf_op jit(solution)/shard_map/finish/pallas_call | solution.py:758

commit v10 on v9

--- a/solution.py
+++ b/solution.py
@@ -89,7 +89,7 @@
     uv, tri, ev, tv, rv, bv, pv, tot, el, av, nt, sp,
     xs, ys, yu, zu, zs, xy, zt, xt, yt,
     rxu, rxs, ryu, rys, rzu, rzs, rxy, rxz, ryz, rt, rtx, rty,
-    in_sem, ready, told, send_sem, recv_sem,
+    in_sem, ready, told, send_sem, recv_sem, spare,
 ):
     X, Y, Z = dims
     N = X * Y
@@ -136,9 +136,7 @@
         copy.start()
 
     def take(sem, rows):
-        whole = [k for k in range(1, 7) if rows % (8 * k) == 0 and rows // k <= N + 2 * Y]
-        planes = whole[0] if whole else rows // 3
-        spot = sp.at[pl.ds(0, planes), pl.ds(0, rows // planes)]
+        spot = sp.at[pl.ds(0, rows // 3), pl.ds(0, 3)] if rows % 8 else spare.at[pl.ds(0, rows)]
         pltpu.make_async_copy(spot, spot, sem).wait()
 
     barrier = pltpu.get_barrier_semaphore()
@@ -207,43 +205,43 @@
     beside = [sum(has[o].astype(jnp.int32) for o in faces[a]) for a in range(3)]
     above, below = me[2], layers - 1 - me[2]
 
-    def products(*ranges):
-        values = {1}
-        for r in ranges:
-            values = {v * w for v in values for w in r}
-        return sorted(values - {0})
-
-    some, any_depth = (1, 2), range(layers)
-    four = products(some, some)
-    arrivals = {
-        "xu": (3 * Y, beside[0], some),
-        "xs": (Y, beside[0] * (8 + above), products(some, [8 + d for d in any_depth])),
-        "yu": (3 * X, beside[1], some),
-        "ys": (X, beside[1] * (8 + above), products(some, [8 + d for d in any_depth])),
-        "zu": (Y, beside[2] + above, sorted({n + d for n in some for d in any_depth})),
-        "zs": (2 * Y, beside[2], some),
-        "xy": (3, beside[0] * beside[1], four),
-        "xz": (3 * Y, beside[0] * beside[2], four),
-        "yz": (2 * W, beside[1] * beside[2], four),
+    places = [
+        (nx, ny, (d > 0) + (d < layers - 1), d)
+        for nx in ((0,), (1,), (1, 2))[min(sizes[0], 3) - 1]
+        for ny in ((0,), (1,), (1, 2))[min(sizes[1], 3) - 1]
+        for d in range(layers)
+    ]
+    own_place = (*beside, above)
+
+    def planes(d):
+        return 7 + jnp.minimum(d, 1) if isinstance(d, jax.Array) else 7 + min(d, 1)
+
+    def early(nx, ny, nz, d):
+        return 3 * X * ny + Y * (nz + d)
+
+    def strike(nx, ny, nz, d):
+        return 3 * Y * nx
+
+    def late(nx, ny, nz, d):
+        return (planes(d) + d) * (Y * nx + X * ny) + 2 * Y * nz + 3 * Y * nx * nz + 2 * W * ny * nz
+
+    def corner(nx, ny, nz, d):
+        return 3 * nx * ny
+
+    def gone(nx, ny, nz, d):
+        down = layers - 1 - d
+        return (planes(d) + 3 + down) * (Y * nx + X * ny) + Y * (3 * nz + down) + 3 * Y * nx * nz + 2 * W * ny * nz
+
+    groups = (early, strike, late, corner)
+    recv_index = {
+        "yu": 0, "zu": 0, "t": 0, "xu": 1, "xs": 2, "ys": 2, "zs": 2, "xz": 2, "yz": 2, "tx": 2, "ty": 2, "xy": 3,
     }
-    departures = (
-        (Y, beside[0] * (11 + below), products(some, [11 + d for d in any_depth])),
-        (X, beside[1] * (11 + below), products(some, [11 + d for d in any_depth])),
-        (Y, 3 * beside[2] + below, sorted({3 * n + d for n in some for d in any_depth})),
-        arrivals["xy"], arrivals["xz"], arrivals["yz"],
-    )
-    recv_index = {kind: i for i, kind in enumerate(arrivals)}
-    recv_index |= {"tx": recv_index["xs"], "ty": recv_index["ys"], "t": recv_index["zu"]}
-    send_index = {
-        "xu": 0, "xs": 0, "tx": 0, "yu": 1, "ys": 1, "ty": 1, "zu": 2, "zs": 2, "t": 2, "xy": 3, "xz": 4, "yz": 5,
-    }
-    sent = [send_sem.at[0], send_sem.at[1], in_sem.at[0], send_sem.at[2], send_sem.at[3], send_sem.at[4]]
     sends = {o: [] for o in offs}
 
-    def message(kind, o, src, dst):
-        sends[o].append((kind, pltpu.make_async_remote_copy(
+    def message(kind, o, src, dst, few=None):
+        sends[o].append((kind if few != 7 else kind + "7", pltpu.make_async_remote_copy(
             src_ref=src, dst_ref=dst,
-            send_sem=sent[send_index[kind]], recv_sem=recv_sem.at[recv_index[kind]],
+            send_sem=send_sem.at[int(kind == "xy")], recv_sem=recv_sem.at[recv_index[kind]],
             device_id=partner(o), device_id_type=MESH,
         )))
 
@@ -252,9 +250,11 @@
         at = (Y, Y * X)[i]
         strike = u_hbm.at[:, pl.ds((0, N - Y)[i], Y), :] if s < 0 else uv.at[:, pl.ds(at, Y), :]
         message("xu", (s, 0, 0), strike, rxu.at[k])
-        message("xs", (s, 0, 0), xs.at[i], rxs.at[k])
+        for few in (7, 8):
+            some = pl.ds(0, few)
+            message("xs", (s, 0, 0), xs.at[i, some], rxs.at[k, some], few)
+            message("ys", (0, s, 0), ys.at[i, some], rys.at[k, some], few)
         message("yu", (0, s, 0), u_rows.at[:, :, 0, :] if s < 0 else yu, ryu.at[k])
-        message("ys", (0, s, 0), ys.at[i], rys.at[k])
         message("zu", (0, 0, s), zu.at[0, pl.ds(0, Y)], rzu.at[k])
         message("zs", (0, 0, s), zs, rzs.at[k])
         for j, s2 in enumerate((-1, 1)):
@@ -270,11 +270,12 @@
     for d in depths:
         message("t", (0, 0, d), zt, rt.at[d - 1])
 
-    def settle(sem, rows, count, values):
-        for n in values:
-            @pl.when(count == n)
+    def settle(sem, group):
+        rows = group(*own_place)
+        for n in sorted({group(*p) for p in places} - {0}):
+            @pl.when(rows == n)
             def _(n=n):
-                take(sem, n * rows)
+                take(sem, n)
 
     def start(offsets_in, kinds):
         for o in offsets_in:
@@ -285,9 +286,8 @@
                     for copy in chosen:
                         copy.start()
 
-    def arrive(*kinds):
-        for kind in kinds:
-            settle(recv_sem.at[recv_index[kind]], *arrivals[kind])
+    def arrive(index):
+        settle(recv_sem.at[index], groups[index])
 
     @pl.when(expected > 0)
     def _():
@@ -415,12 +415,12 @@
             xt[i] = tot[pl.ds(at * Y, Y), :]
             yt[i] = tot[pl.ds(line, X, stride=Y), :]
 
-    def along_dip():
+    def along_dip(kind):
         for i, line in enumerate((0, Y - 1)):
             for k in range(8):
                 src = el.at[k] if k < 6 else (av, nt)[k - 6]
                 ys[i, k] = src[pl.ds(line, X, stride=Y), :]
-        start(lowers, ("ys",))
+        start(lowers, (kind,))
 
     @pl.when(above == 0)
     def _():
@@ -431,7 +431,7 @@
         for x in ends:
             elastic(x, None)
             factors(x, None)
-        start(lowers, ("xs",))
+        start(lowers, ("xs7",))
         prefix(inner)
         for x in inner:
             strain(x)
@@ -439,7 +439,7 @@
         for x in inner:
             elastic(x, None)
             factors(x, None)
-        along_dip()
+        along_dip("ys7")
         pack_displacement()
         lines_along_depth()
         total_tiles()
@@ -474,7 +474,7 @@
         for k in range(2):
             zs[k] = tiles[k]
         start(lowers, ("zs", "t", "tx", "ty"))
-        along_dip()
+        along_dip("ys")
 
     near = [o for o in uppers if sum(o) == 1]
     number = sum(has[o].astype(jnp.int32) for o in near)
@@ -505,14 +505,18 @@
         start(offsets_in, diagonal)
 
     hear(close, told.at[0])
-    start(near, ("ys", "xs"))
+    for kinds, deeper in ((("ys7", "xs7"), False), (("ys", "xs"), True)):
+        @pl.when((above > 0) if deeper else (above == 0))
+        def _(kinds=kinds):
+            start(near, kinds)
+
     hear(others, ready.at[1])
     for o in far:
         announce(o)
     if far:
         hear(far, told.at[1])
 
-    arrive("yu")
+    arrive(0)
     for side, line in enumerate((0, Y - 1)):
         sign = 2.0 * side - 1.0
 
@@ -522,7 +526,6 @@
             for c, (part, factor) in enumerate(TERMS[1]):
                 el[part, own, :] = el[part, own, :] + (sign * factor) * ryu[side, c]
 
-    arrive("zu")
     carried = plane
     for d in depths:
         carried = carried + rt[d - 1]
@@ -542,7 +545,7 @@
     for x in range(X):
         if x not in ends:
             advance(x)
-    arrive("xu")
+    arrive(1)
     for side, at in enumerate((0, X - 1)):
         sign = 2.0 * side - 1.0
 
@@ -577,11 +580,12 @@
     def ends_of(first, last, rows, count):
         return jnp.where(rows == 0, -first, jnp.where(rows == count - 1, last, 0.0))
 
-    arrive("xy", "yz", "xz", "ys", "zs", "xs")
+    arrive(2)
+    arrive(3)
 
     def beyond(axis, side, part):
         got, load, e = part
-        trace, change = flow(e, got[6] * jnp.exp(load * got[7]))
+        trace, change = flow(e, got[6] * jnp.exp(jnp.where(above > 0, load * got[7], 0.0)))
         there = has[faces[axis][side]]
         return [
             (side - 0.5) * jnp.where(there, stress(e, change, trace, k), 0.0) for k in (X_SET, Y_SET)[axis]
@@ -670,8 +674,8 @@
             own = pl.ds(line, X, stride=Y)
             mv[c, own, :] = mv[c, own, :] + along_y[side][c]
 
-    for i, departure in enumerate(departures):
-        settle(sent[i], *departure)
+    settle(send_sem.at[0], gone)
+    settle(send_sem.at[1], corner)
 
 
 def finish(dims, fv, mv, jv, f_hbm, m_hbm, ms, sem):
@@ -749,8 +753,9 @@
             dma((3,)),
             pltpu.SemaphoreType.REGULAR((2,)),
             pltpu.SemaphoreType.REGULAR((1 if layers == 2 else 2,)),
-            dma((5,)),
-            dma((9,)),
+            dma((2,)),
+            dma((4,)),
+            vmem(((11 + layers) * 2 * (X + Y) + (18 + layers) * Y + 8 * W, Z), f32),
         ],
         compiler_params=pltpu.CompilerParams(collective_id=0, has_side_effects=True),
         name="strain_step",

time: 9.33 us -> 9.24 us (level)
  no operation moved by 1% of the time
where the time goes in v10:
time: 9.24 us; the launch traced here: 9.09 us
  Pallas kernels  8.45 us (91%)
  between operations  0.64 us (7%)
    pallas_call x1, Pallas kernels, shards(): pl.pallas_call(functools.partial(kernel, (X, Y, Z), sizes), out_shape=(vm...  7.41 us
    pallas_call x1, Pallas kernels, shards(): pl.pallas_call(functools.partial(finish, (X, Y, Z)), out_shape=(jax.Shape...  1.04 us

profile of v10, /device:TPU:0, one launch (start us, length us, event | category | flops | bytes accessed | tf_op | source)
XLA Modules:
  0.0 9.1 jit_solution(3401224209866240070)
XLA Ops:
  0.6 7.4 %strain_step.1 = (f32[6,256,128]{2,1,0:T(8,128)S(1)}, f32[3,256,128]{2,1,0:T(8,128)S(1)}, f32[16,128]{1,0:T(8,128)S(1)}) custom-call(f32[3,256,128]{2,1,0:T(8,128)} %bitcast.7, f32[3,16,16,128]{3,2,1,0:T(8,128)} %u_rows.1, f32[6,256,128]{2,1,0:T(8,128)} %bitcast.8, f32[256,128]{1,0:T(8,128)} %bitcast.9, f32[256,128]{1,0:T(8,128)} %bitcast.10, ...), custom_call_target="tpu_custom_call" | custom-call | tf_op jit(solution)/shard_map/strain_step/pallas_call | solution.py:714
  8.0 1.0 %finish.1 = (f32[6,256,128]{2,1,0:T(8,128)}, f32[3,256,128]{2,1,0:T(8,128)}) custom-call(f32[6,256,128]{2,1,0:T(8,128)S(1)} %get-tuple-element.7.fv, f32[3,256,128]{2,1,0:T(8,128)S(1)} %get-tuple-element.8.mv, f32[16,128]{1,0:T(8,128)S(1)} %get-tuple-element.9.jv), custom_call_target="tpu_custom_call" | custom-call | tf_op jit(solution)/shard_map/finish/pallas_call | solution.py:763

commit v11 on v10

--- a/solution.py
+++ b/solution.py
@@ -85,8 +85,8 @@
 def kernel(
     dims, sizes,
     u_hbm, u_rows, e_hbm, t_hbm, r_hbm, b_hbm,
-    fv, mv, jv,
-    uv, tri, ev, tv, rv, bv, pv, tot, el, av, nt, sp,
+    fv, mv, jv, dv,
+    uv, tri, zown, ev, tv, rv, bv, pv, tot, el, av, nt, sp,
     xs, ys, yu, zu, zs, xy, zt, xt, yt,
     rxu, rxs, ryu, rys, rzu, rzs, rxy, rxz, ryz, rt, rtx, rty,
     in_sem, ready, told, send_sem, recv_sem, spare,
@@ -254,7 +254,7 @@
             some = pl.ds(0, few)
             message("xs", (s, 0, 0), xs.at[i, some], rxs.at[k, some], few)
             message("ys", (0, s, 0), ys.at[i, some], rys.at[k, some], few)
-        message("yu", (0, s, 0), u_rows.at[:, :, 0, :] if s < 0 else yu, ryu.at[k])
+        message("yu", (0, s, 0), u_rows.at[:, :, 0, :] if s < 0 else yu.at[1], ryu.at[k])
         message("zu", (0, 0, s), zu.at[0, pl.ds(0, Y)], rzu.at[k])
         message("zs", (0, 0, s), zs, rzs.at[k])
         for j, s2 in enumerate((-1, 1)):
@@ -399,8 +399,7 @@
             for c in range(3):
                 p = 3 * i + c
                 lines = uv[c, pl.ds(Y + line, X, stride=Y), :]
-                if i:
-                    yu[c] = lines
+                yu[i, c] = lines
                 tile = jnp.where(pair_x == p, pltpu.roll(lines, (2 * p + 1) % Z, 1), tile)
                 for j, at in enumerate((0, X - 1)):
                     xy[j, i, pl.ds(c, 1), :] = uv[c, pl.ds(Y + at * Y + line, 1), :]
@@ -516,6 +515,16 @@
     if far:
         hear(far, told.at[1])
 
+    block = 2 * X
+
+    def shift(tile, by):
+        return pltpu.roll(tile, by % Z, 1) if by % Z else tile
+
+    mine = zu[0, pl.ds(0, Y), :]
+    from_z = jnp.where(even, shift(mine, -1), -shift(mine, 1))
+    for c in range(3):
+        zown[c] = shift(from_z, -c * block)
+
     arrive(0)
     for side, line in enumerate((0, Y - 1)):
         sign = 2.0 * side - 1.0
@@ -591,10 +600,9 @@
             (side - 0.5) * jnp.where(there, stress(e, change, trace, k), 0.0) for k in (X_SET, Y_SET)[axis]
         ]
 
-    along_y = []
-    for side, line in enumerate((0, Y - 1)):
+    for side in range(2):
         e = [rys[side, k] for k in range(6)]
-        add(e, 1, 1.0 - 2.0 * side, [uv[c, pl.ds(Y + line, X, stride=Y), :] for c in range(3)])
+        add(e, 1, 1.0 - 2.0 * side, [yu[side, c] for c in range(3)])
         add(e, 0, 1.0, [
             ends_of(rxy[0, side, pl.ds(c, 1), :], rxy[1, side, pl.ds(c, 1), :], row_x, X) for c in range(3)
         ])
@@ -603,7 +611,8 @@
         load = row_plane
         for d in depths:
             load = load + rty[side, d - 1]
-        along_y.append(beyond(1, side, (rys[side], load, e)))
+        for c, tile in enumerate(beyond(1, side, (rys[side], load, e))):
+            dv[side, c] = tile
 
     along_x = []
     for side, at in enumerate((0, X - 1)):
@@ -624,15 +633,8 @@
             load = load + rtx[side, d - 1]
         along_x.append(beyond(0, side, (rxs[side], load, e)))
 
-    block = 2 * X
-
-    def shift(tile, by):
-        return pltpu.roll(tile, by % Z, 1) if by % Z else tile
-
     halo = [jnp.where(even, rzs[0, k], rzs[1, k]) for k in range(2)]
     parts = [shift(halo[k // 4], -(k % 4) * block) for k in range(8)]
-    mine = zu[0, pl.ds(0, Y), :]
-    from_z = jnp.where(even, shift(mine, -1), -shift(mine, 1))
     from_x = []
     for c in range(3):
         left, right = (jnp.where(lane == Z - 1, rxz[i, 0, c], rxz[i, 1, c]) for i in range(2))
@@ -647,8 +649,8 @@
     )
     e = list(parts[:6])
     add(e, 0, 1.0, from_x)
-    for axis, tile in ((1, from_y), (2, from_z)):
-        add(e, axis, 1.0, [shift(tile, -c * block) for c in range(3)])
+    add(e, 1, 1.0, [shift(from_y, -c * block) for c in range(3)])
+    add(e, 2, 1.0, [zown[c] for c in range(3)])
     deeper = plane
     for d in depths:
         if d >= 2:
@@ -660,38 +662,35 @@
         has[0, 0, -1].astype(jnp.float32),
         has[0, 0, 1].astype(jnp.float32),
     )
-    gathered = plane
     for c in range(3):
-        tile = shift(stress(e, change, trace, Z_SET[c]) * known, c * block)
-        gathered = jnp.where((pair >= c * X) & (pair < (c + 1) * X), tile, gathered)
-    jv[...] = jnp.where(even, gathered, shift(gathered, -2))
+        jv[c] = jnp.where(pair < X, stress(e, change, trace, Z_SET[c]) * known, 0.0)
 
     for c in range(3):
         for side, at in enumerate((0, X - 1)):
             own = pl.ds(at * Y, Y)
             mv[c, own, :] = mv[c, own, :] + along_x[side][c]
-        for side, line in enumerate((0, Y - 1)):
-            own = pl.ds(line, X, stride=Y)
-            mv[c, own, :] = mv[c, own, :] + along_y[side][c]
 
     settle(send_sem.at[0], gone)
     settle(send_sem.at[1], corner)
 
 
-def finish(dims, fv, mv, jv, f_hbm, m_hbm, ms, sem):
+def finish(dims, fv, mv, jv, dv, f_hbm, m_hbm, ms, sem):
     X, Y, Z = dims
     copies = [pltpu.make_async_copy(fv, f_hbm, sem.at[0])]
     copies[0].start()
     lane = lax.broadcasted_iota(jnp.int32, (Y, Z), 1)
     z_edge = jnp.where(lane == 0, -0.5, jnp.where(lane == Z - 1, 0.5, 0.0)).astype(jnp.float32)
-    joined = jv[...]
+    row = lax.broadcasted_iota(jnp.int32, (Y, Z), 0)
+    joined = [merge(jv[c], jv[c]) for c in range(3)]
     groups = 4
     span = X // groups
     for g in range(groups):
         for x in range(g * span, (g + 1) * span):
             own = pl.ds(x * Y, Y)
             for c in range(3):
-                ms[c, own, :] = mv[c, own, :] + edge_term(joined, c * X + x, z_edge)
+                first, last = (dv[side, c, pl.ds(x, 1), :] for side in range(2))
+                edge = jnp.where(row == 0, first, jnp.where(row == Y - 1, last, 0.0))
+                ms[c, own, :] = mv[c, own, :] + edge + edge_term(joined[c], x, z_edge)
         rows = pl.ds(g * span * Y, span * Y)
         copies.append(pltpu.make_async_copy(ms.at[:, rows, :], m_hbm.at[:, rows, :], sem.at[1 + g]))
         copies[-1].start()
@@ -713,12 +712,13 @@
     D = max(layers - 1, 1)
     kept = pl.pallas_call(
         functools.partial(kernel, (X, Y, Z), sizes),
-        out_shape=(vmem((6, N, Z), f32), vmem((3, N, Z), f32), vmem((Y, Z), f32)),
+        out_shape=(vmem((6, N, Z), f32), vmem((3, N, Z), f32), vmem((3, Y, Z), f32), vmem((2, 3, X, Z), f32)),
         in_specs=[any_space] * 6,
-        out_specs=(in_vmem,) * 3,
+        out_specs=(in_vmem,) * 4,
         scratch_shapes=[
             vmem((3, N + 2 * Y, Z), f32),
             vmem((Z, 2 * Z), jnp.bfloat16),
+            vmem((3, Y, Z), f32),
             vmem((6, N, Z), f32),
             vmem((N, Z), f32),
             vmem((N, Z), f32),
@@ -731,7 +731,7 @@
             vmem((6, N + 2 * Y, Z), f32),
             vmem((2, 8, Y, Z), f32),
             vmem((2, 8, X, Z), f32),
-            vmem((3, X, Z), f32),
+            vmem((2, 3, X, Z), f32),
             vmem((2, W, Z), f32),
             vmem((2, Y, Z), f32),
             vmem((2, 2, 8, Z), f32),
@@ -763,7 +763,7 @@
     f, m = pl.pallas_call(
         functools.partial(finish, (X, Y, Z)),
         out_shape=(jax.ShapeDtypeStruct((6, N, Z), f32), jax.ShapeDtypeStruct((3, N, Z), f32)),
-        in_specs=[in_vmem] * 3,
+        in_specs=[in_vmem] * 4,
         out_specs=(any_space, any_space),
         scratch_shapes=[vmem((3, N, Z), f32), dma((5,))],
         name="finish",

time: 9.24 us -> 9.12 us (0.987)
  Pallas kernels: 8.45 us -> 8.34 us
    pallas_call x1, Pallas kernels: 7.41 us -> 7.29 us  [shards(): pl.pallas_call(functools.partial(kernel, (X, Y, Z), sizes), out_shape=(vm...]
where the time goes in v11:
time: 9.12 us; the launch traced here: 8.98 us
  Pallas kernels  8.34 us (91%)
  between operations  0.64 us (7%)
    pallas_call x1, Pallas kernels, shards(): pl.pallas_call(functools.partial(kernel, (X, Y, Z), sizes), out_shape=(vm...  7.29 us
    pallas_call x1, Pallas kernels, shards(): pl.pallas_call(functools.partial(finish, (X, Y, Z)), out_shape=(jax.Shape...  1.04 us

profile of v11, /device:TPU:0, one launch (start us, length us, event | category | flops | bytes accessed | tf_op | source)
XLA Modules:
  0.0 9.0 jit_solution(2345815237787710172)
XLA Ops:
  0.6 7.3 %strain_step.1 = (f32[6,256,128]{2,1,0:T(8,128)S(1)}, f32[3,256,128]{2,1,0:T(8,128)S(1)}, f32[3,16,128]{2,1,0:T(8,128)S(1)}, f32[2,3,16,128]{3,2,1,0:T(8,128)S(1)}) custom-call(f32[3,256,128]{2,1,0:T(8,128)} %bitcast.7, f32[3,16,16,128]{3,2,1,0:T(8,128)} %u_rows.1, f32[6,256,128]{2,1,0:T(8,128)} %bitcast.8, f32[256,128]{1,0:T(8,128)} %bitcast.9, ...), custom_call_target="tpu_custom_call" | custom-call | tf_op jit(solution)/shard_map/strain_step/pallas_call | solution.py:713
  7.9 1.0 %finish.1 = (f32[6,256,128]{2,1,0:T(8,128)}, f32[3,256,128]{2,1,0:T(8,128)}) custom-call(f32[6,256,128]{2,1,0:T(8,128)S(1)} %get-tuple-element.8.fv, f32[3,256,128]{2,1,0:T(8,128)S(1)} %get-tuple-element.9.mv, f32[3,16,128]{2,1,0:T(8,128)S(1)} %get-tuple-element.10.jv, f32[2,3,16,128]{3,2,1,0:T(8,128)S(1)} %get-tuple-element.11.dv), custom_call_target="tpu_custom_call" | custom-call | tf_op jit(solution)/shard_map/finish/pallas_call | solution.py:763

commit v12 on v11

--- a/solution.py
+++ b/solution.py
@@ -216,11 +216,11 @@
     def planes(d):
         return 7 + jnp.minimum(d, 1) if isinstance(d, jax.Array) else 7 + min(d, 1)
 
-    def early(nx, ny, nz, d):
-        return 3 * X * ny + Y * (nz + d)
-
-    def strike(nx, ny, nz, d):
-        return 3 * Y * nx
+    def sides(nx, ny, nz, d):
+        return 3 * X * ny + 3 * Y * nx
+
+    def depths_of(nx, ny, nz, d):
+        return Y * (nz + d)
 
     def late(nx, ny, nz, d):
         return (planes(d) + d) * (Y * nx + X * ny) + 2 * Y * nz + 3 * Y * nx * nz + 2 * W * ny * nz
@@ -232,9 +232,9 @@
         down = layers - 1 - d
         return (planes(d) + 3 + down) * (Y * nx + X * ny) + Y * (3 * nz + down) + 3 * Y * nx * nz + 2 * W * ny * nz
 
-    groups = (early, strike, late, corner)
+    groups = (sides, depths_of, late, corner)
     recv_index = {
-        "yu": 0, "zu": 0, "t": 0, "xu": 1, "xs": 2, "ys": 2, "zs": 2, "xz": 2, "yz": 2, "tx": 2, "ty": 2, "xy": 3,
+        "yu": 0, "xu": 0, "zu": 1, "t": 1, "xs": 2, "ys": 2, "zs": 2, "xz": 2, "yz": 2, "tx": 2, "ty": 2, "xy": 3,
     }
     sends = {o: [] for o in offs}
 
@@ -457,7 +457,6 @@
         lines_along_depth()
         start(lowers, ("yz",))
         prefix(range(X))
-        total_tiles()
         for x in range(X):
             strain(x)
         take(in_sem.at[1], 12 * Y + 2 * N)
@@ -472,8 +471,10 @@
             factors(x, tiles)
         for k in range(2):
             zs[k] = tiles[k]
-        start(lowers, ("zs", "t", "tx", "ty"))
+        start(lowers, ("zs",))
         along_dip("ys")
+        total_tiles()
+        start(lowers, ("t", "tx", "ty"))
 
     near = [o for o in uppers if sum(o) == 1]
     number = sum(has[o].astype(jnp.int32) for o in near)
@@ -535,6 +536,16 @@
             for c, (part, factor) in enumerate(TERMS[1]):
                 el[part, own, :] = el[part, own, :] + (sign * factor) * ryu[side, c]
 
+    for side, at in enumerate((0, X - 1)):
+        sign = 2.0 * side - 1.0
+
+        @pl.when(has[faces[0][side]])
+        def _(side=side, sign=sign, at=at):
+            own = pl.ds(at * Y, Y)
+            for c, (part, factor) in enumerate(TERMS[0]):
+                el[part, own, :] = el[part, own, :] + (sign * factor) * rxu[side, c]
+
+    arrive(1)
     carried = plane
     for d in depths:
         carried = carried + rt[d - 1]
@@ -552,19 +563,6 @@
             sp[c, pl.ds(Y + x * Y, Y), :] = stress(e, change, trace, c)
 
     for x in range(X):
-        if x not in ends:
-            advance(x)
-    arrive(1)
-    for side, at in enumerate((0, X - 1)):
-        sign = 2.0 * side - 1.0
-
-        @pl.when(has[faces[0][side]])
-        def _(side=side, sign=sign, at=at):
-            own = pl.ds(at * Y, Y)
-            for c, (part, factor) in enumerate(TERMS[0]):
-                el[part, own, :] = el[part, own, :] + (sign * factor) * rxu[side, c]
-
-    for x in ends:
         advance(x)
 
     for x in range(X):

time: 9.12 us -> 9.13 us (level)
  no operation moved by 1% of the time
where the time goes in v12:
time: 9.13 us; the launch traced here: 8.98 us
  Pallas kernels  8.34 us (91%)
  between operations  0.64 us (7%)
    pallas_call x1, Pallas kernels, shards(): pl.pallas_call(functools.partial(kernel, (X, Y, Z), sizes), out_shape=(vm...  7.3 us
    pallas_call x1, Pallas kernels, shards(): pl.pallas_call(functools.partial(finish, (X, Y, Z)), out_shape=(jax.Shape...  1.04 us

profile of v12, /device:TPU:0, one launch (start us, length us, event | category | flops | bytes accessed | tf_op | source)
XLA Modules:
  0.0 9.0 jit_solution(1204368295167487092)
XLA Ops:
  0.6 7.3 %strain_step.1 = (f32[6,256,128]{2,1,0:T(8,128)S(1)}, f32[3,256,128]{2,1,0:T(8,128)S(1)}, f32[3,16,128]{2,1,0:T(8,128)S(1)}, f32[2,3,16,128]{3,2,1,0:T(8,128)S(1)}) custom-call(f32[3,256,128]{2,1,0:T(8,128)} %bitcast.7, f32[3,16,16,128]{3,2,1,0:T(8,128)} %u_rows.1, f32[6,256,128]{2,1,0:T(8,128)} %bitcast.8, f32[256,128]{1,0:T(8,128)} %bitcast.9, ...), custom_call_target="tpu_custom_call" | custom-call | tf_op jit(solution)/shard_map/strain_step/pallas_call | solution.py:711
  7.9 1.0 %finish.1 = (f32[6,256,128]{2,1,0:T(8,128)}, f32[3,256,128]{2,1,0:T(8,128)}) custom-call(f32[6,256,128]{2,1,0:T(8,128)S(1)} %get-tuple-element.8.fv, f32[3,256,128]{2,1,0:T(8,128)S(1)} %get-tuple-element.9.mv, f32[3,16,128]{2,1,0:T(8,128)S(1)} %get-tuple-element.10.jv, f32[2,3,16,128]{3,2,1,0:T(8,128)S(1)} %get-tuple-element.11.dv), custom_call_target="tpu_custom_call" | custom-call | tf_op jit(solution)/shard_map/finish/pallas_call | solution.py:761

commit v13 on v12

--- a/solution.py
+++ b/solution.py
@@ -136,7 +136,7 @@
         copy.start()
 
     def take(sem, rows):
-        spot = sp.at[pl.ds(0, rows // 3), pl.ds(0, 3)] if rows % 8 else spare.at[pl.ds(0, rows)]
+        spot = spare.at[pl.ds(0, rows)]
         pltpu.make_async_copy(spot, spot, sem).wait()
 
     barrier = pltpu.get_barrier_semaphore()
@@ -222,26 +222,26 @@
     def depths_of(nx, ny, nz, d):
         return Y * (nz + d)
 
+    def corners(nx, ny, nz):
+        return 3 * nx * ny + 3 * Y * nx * nz + 2 * W * ny * nz
+
     def late(nx, ny, nz, d):
-        return (planes(d) + d) * (Y * nx + X * ny) + 2 * Y * nz + 3 * Y * nx * nz + 2 * W * ny * nz
-
-    def corner(nx, ny, nz, d):
-        return 3 * nx * ny
+        return (planes(d) + d) * (Y * nx + X * ny) + 2 * Y * nz + corners(nx, ny, nz)
 
     def gone(nx, ny, nz, d):
         down = layers - 1 - d
-        return (planes(d) + 3 + down) * (Y * nx + X * ny) + Y * (3 * nz + down) + 3 * Y * nx * nz + 2 * W * ny * nz
-
-    groups = (sides, depths_of, late, corner)
+        return (planes(d) + 3 + down) * (Y * nx + X * ny) + Y * (3 * nz + down) + corners(nx, ny, nz)
+
+    groups = (sides, depths_of, late)
     recv_index = {
-        "yu": 0, "xu": 0, "zu": 1, "t": 1, "xs": 2, "ys": 2, "zs": 2, "xz": 2, "yz": 2, "tx": 2, "ty": 2, "xy": 3,
+        "yu": 0, "xu": 0, "zu": 1, "t": 1, "xs": 2, "ys": 2, "zs": 2, "xz": 2, "yz": 2, "tx": 2, "ty": 2, "xy": 2,
     }
     sends = {o: [] for o in offs}
 
     def message(kind, o, src, dst, few=None):
         sends[o].append((kind if few != 7 else kind + "7", pltpu.make_async_remote_copy(
             src_ref=src, dst_ref=dst,
-            send_sem=send_sem.at[int(kind == "xy")], recv_sem=recv_sem.at[recv_index[kind]],
+            send_sem=send_sem.at[0], recv_sem=recv_sem.at[recv_index[kind]],
             device_id=partner(o), device_id_type=MESH,
         )))
 
@@ -588,7 +588,6 @@
         return jnp.where(rows == 0, -first, jnp.where(rows == count - 1, last, 0.0))
 
     arrive(2)
-    arrive(3)
 
     def beyond(axis, side, part):
         got, load, e = part
@@ -669,7 +668,6 @@
             mv[c, own, :] = mv[c, own, :] + along_x[side][c]
 
     settle(send_sem.at[0], gone)
-    settle(send_sem.at[1], corner)
 
 
 def finish(dims, fv, mv, jv, dv, f_hbm, m_hbm, ms, sem):
@@ -751,8 +749,8 @@
             dma((3,)),
             pltpu.SemaphoreType.REGULAR((2,)),
             pltpu.SemaphoreType.REGULAR((1 if layers == 2 else 2,)),
-            dma((2,)),
-            dma((4,)),
+            dma((1,)),
+            dma((3,)),
             vmem(((11 + layers) * 2 * (X + Y) + (18 + layers) * Y + 8 * W, Z), f32),
         ],
         compiler_params=pltpu.CompilerParams(collective_id=0, has_side_effects=True),

time: 9.13 us -> 9.11 us (level)
  no operation moved by 1% of the time
where the time goes in v13:
time: 9.11 us; the launch traced here: 8.96 us
  Pallas kernels  8.32 us (91%)
  between operations  0.64 us (7%)
    pallas_call x1, Pallas kernels, shards(): pl.pallas_call(functools.partial(kernel, (X, Y, Z), sizes), out_shape=(vm...  7.28 us
    pallas_call x1, Pallas kernels, shards(): pl.pallas_call(functools.partial(finish, (X, Y, Z)), out_shape=(jax.Shape...  1.04 us

profile of v13, /device:TPU:0, one launch (start us, length us, event | category | flops | bytes accessed | tf_op | source)
XLA Modules:
  0.0 9.0 jit_solution(15052005651767774918)
XLA Ops:
  0.6 7.3 %strain_step.1 = (f32[6,256,128]{2,1,0:T(8,128)S(1)}, f32[3,256,128]{2,1,0:T(8,128)S(1)}, f32[3,16,128]{2,1,0:T(8,128)S(1)}, f32[2,3,16,128]{3,2,1,0:T(8,128)S(1)}) custom-call(f32[3,256,128]{2,1,0:T(8,128)} %bitcast.7, f32[3,16,16,128]{3,2,1,0:T(8,128)} %u_rows.1, f32[6,256,128]{2,1,0:T(8,128)} %bitcast.8, f32[256,128]{1,0:T(8,128)} %bitcast.9, ...), custom_call_target="tpu_custom_call" | custom-call | tf_op jit(solution)/shard_map/strain_step/pallas_call | solution.py:709
  7.9 1.0 %finish.1 = (f32[6,256,128]{2,1,0:T(8,128)}, f32[3,256,128]{2,1,0:T(8,128)}) custom-call(f32[6,256,128]{2,1,0:T(8,128)S(1)} %get-tuple-element.8.fv, f32[3,256,128]{2,1,0:T(8,128)S(1)} %get-tuple-element.9.mv, f32[3,16,128]{2,1,0:T(8,128)S(1)} %get-tuple-element.10.jv, f32[2,3,16,128]{3,2,1,0:T(8,128)S(1)} %get-tuple-element.11.dv), custom_call_target="tpu_custom_call" | custom-call | tf_op jit(solution)/shard_map/finish/pallas_call | solution.py:759
